TPU v7x, 768 devices: a whole 4x8x12 slice. The times are simulated.
768 devices in a mesh: gx: 96 (over y, z), gy: 8 (over x, core).
Axes of the slice: x: 4, y: 8, z: 12, core: 2. Of those that a mesh axis runs over, the one named last changes fastest.
Arguments:
- component_share_field: float32 [32, 768, 64, 128], P(None, 'gx', 'gy'), may hold values from 0.05 to 1
- scaled_heat_level: float32 [768, 64, 128], P('gx', 'gy'), may hold values from 1 to 2.5
- local_transport_value: float32 [768, 64, 128], P('gx', 'gy'), may hold values from 0.5 to 2
- component_spreading_scale: float32 [16], replicated, may hold values from 0.1 to 1
- screened_poisson_reactive_term: float32 [16], replicated, may hold values from 0.5 to 4
- expansion_contribution_scale: float32 [32], replicated, may hold values from -3 to 3
- logarithm_arrhenius_constant: float32 [128], replicated, may hold values from -3 to -1
- arrhenius_energy_scale: float32 [128], replicated, may hold values from 0 to 4
- kinetic_exponents: int32 [128, 32], replicated, may hold values 0 or 1
- reaction_change_matrix: int32 [32, 128], replicated, may hold values from -1 to 1
Outputs:
- species_new: float32 [16, 768, 64, 128], P(None, 'gx', 'gy')
- div_field: float32 [768, 64, 128], P('gx', 'gy')
Inputs may be any that keep to these rules, and one draw needn't show every extreme that they name: `reaction_change_matrix`: each entry is -1, 0 or 1.
All inputs are finite; a program needn't handle non-finite values.
Results may differ from a plain program's by a relative error of at most 0.0001.
Values sent between devices are 32-bit elements; how exact they have to be, the bound alone decides.
A program may use at most 32 MiB of HBM per device.

v0:
```python
import jax
import jax.numpy as jnp
import numpy as np
from jax import lax
from jax.sharding import Mesh
from jax.sharding import PartitionSpec as P

GX_GY = ("gx_0", "gx_1", "gy_0", "gy_1")
GX = ("gx_0", "gx_1")
GY = ("gy_0", "gy_1")


def padded_2(block, sides, width):
    for axis, dim in sides:
        count = lax.axis_size(axis)
        forward = [(i, i + 1) for i in range(count - 1)]
        forward.append((count - 1, 0))
        backward = [(target, source) for source, target in forward]
        low = lax.ppermute(
            lax.slice_in_dim(block, block.shape[dim] - width, None, axis=dim), axis, forward
        )
        high = lax.ppermute(lax.slice_in_dim(block, 0, width, axis=dim), axis, backward)
        block = jnp.concatenate([low, block, high], axis=dim)
    return block


def over_axes(array, axes):
    for axis in axes:
        array = lax.psum(array, axis)
    return array


def legendre_seven(points):
    return (429.0 * points**7 - 693.0 * points**5 + 315.0 * points**3 - 35.0 * points) / 16.0


def gll_tables():
    gll_nodes = np.array(
        [
            -1.0,
            -0.8717401485096066,
            -0.5917001814331423,
            -0.2092992179024789,
            0.2092992179024789,
            0.5917001814331423,
            0.8717401485096066,
            1.0,
        ]
    )
    at_nodes = legendre_seven(gll_nodes)
    weights = 2.0 / (56.0 * at_nodes * at_nodes)
    derivative = np.zeros((8, 8))
    for row_index in range(8):
        for col_index in range(8):
            if row_index != col_index:
                derivative[row_index, col_index] = at_nodes[row_index] / (
                    at_nodes[col_index] * (gll_nodes[row_index] - gll_nodes[col_index])
                )
    derivative[0, 0] = -14.0
    derivative[7, 7] = 14.0
    return (derivative, weights)


def mass_weights(size_x, size_y, size_z, weights):
    table = jnp.asarray(weights, jnp.float32)
    along_one = jnp.tile(table, size_x // 8)
    along_two = jnp.tile(table, size_y // 8)
    along_three = jnp.tile(table, size_z // 8)
    return along_one[:, None, None] * along_two[None, :, None] * along_three[None, None, :]


def multiplicities(size_x, size_y, size_z):
    table = jnp.asarray(np.array([2.0, 1, 1, 1, 1, 1, 1, 2.0]), jnp.float32)
    along_one = jnp.tile(table, size_x // 8)
    along_two = jnp.tile(table, size_y // 8)
    along_three = jnp.tile(table, size_z // 8)
    return along_one[:, None, None] * along_two[None, :, None] * along_three[None, None, :]


def along_x(values, matrix):
    count_s, size_x, size_y, size_z = values.shape
    blocks = values.reshape(count_s, size_x // 8, 8, size_y, size_z)
    result = jnp.einsum("ij,aejyz->aeiyz", matrix, blocks, precision=lax.Precision.HIGHEST)
    return result.reshape(count_s, size_x, size_y, size_z)


def along_y(values, matrix):
    count_s, size_x, size_y, size_z = values.shape
    blocks = values.reshape(count_s, size_x, size_y // 8, 8, size_z)
    result = jnp.einsum("ij,axejz->axeiz", matrix, blocks, precision=lax.Precision.HIGHEST)
    return result.reshape(count_s, size_x, size_y, size_z)


def along_z(values, matrix):
    size_z = values.shape[3]
    block_deriv = jnp.kron(jnp.eye(size_z // 8, dtype=jnp.float32), matrix)
    return jnp.dot(values, block_deriv.T, precision=lax.Precision.HIGHEST)


def stiffness(values, weighted_cond, deriv_mat):
    trans_mat = deriv_mat.T
    stiff_sum = along_x(weighted_cond * along_x(values, deriv_mat), trans_mat)
    stiff_sum = stiff_sum + along_y(weighted_cond * along_y(values, deriv_mat), trans_mat)
    return stiff_sum + along_z(weighted_cond * along_z(values, deriv_mat), trans_mat)


def diag_stiffness(weighted_cond, deriv_mat):
    square_t = (deriv_mat * deriv_mat).T
    source = weighted_cond[None]
    return along_x(source, square_t) + along_y(source, square_t) + along_z(source, square_t)


def reaction_speeds(
    fractions,
    temps,
    kinetic_exponents_float,
    change_matrix_float,
    logarithm_arrhenius_constant,
    arrhenius_energy_scale,
):
    species_all = fractions.shape[0]
    log_frac = jnp.log(fractions).reshape(species_all, -1)
    exponent = (
        jnp.dot(kinetic_exponents_float, log_frac, precision=lax.Precision.HIGHEST)
        + logarithm_arrhenius_constant[:, None]
        - arrhenius_energy_scale[:, None] * (1.0 / temps.reshape(1, -1) - 1.0)
    )
    progress = jnp.exp(exponent)
    return jnp.dot(change_matrix_float, progress, precision=lax.Precision.HIGHEST).reshape(
        fractions.shape
    )


def fold_rims(padded):
    count_s, pad_x, pad_y, size_z = padded.shape
    size_x = pad_x - 2
    size_y = pad_y - 2
    pos_x = jnp.arange(size_x) % 8
    low_x = (pos_x == 0)[None, :, None, None]
    high_x = (pos_x == 7)[None, :, None, None]
    summed = (
        padded[:, 1:-1]
        + jnp.where(low_x, padded[:, :-2], 0.0)
        + jnp.where(high_x, padded[:, 2:], 0.0)
    )
    pos_y = jnp.arange(size_y) % 8
    low_y = (pos_y == 0)[None, None, :, None]
    high_y = (pos_y == 7)[None, None, :, None]
    summed = (
        summed[:, :, 1:-1]
        + jnp.where(low_y, summed[:, :, :-2], 0.0)
        + jnp.where(high_y, summed[:, :, 2:], 0.0)
    )
    pos_z = jnp.arange(size_z) % 8
    low_z = (pos_z == 0)[None, None, None, :]
    high_z = (pos_z == 7)[None, None, None, :]
    return (
        summed
        + jnp.where(low_z, jnp.roll(summed, 1, 3), 0.0)
        + jnp.where(high_z, jnp.roll(summed, -1, 3), 0.0)
    )


def shards(
    component_share_field,
    scaled_heat_level,
    local_transport_value,
    component_spreading_scale,
    screened_poisson_reactive_term,
    expansion_contribution_scale,
    logarithm_arrhenius_constant,
    arrhenius_energy_scale,
    kinetic_exponents,
    reaction_change_matrix,
):
    derivative, weights = gll_tables()
    deriv_mat = jnp.asarray(derivative, jnp.float32)
    species_all, size_x, size_y, size_z = component_share_field.shape
    species_solved = component_spreading_scale.shape[0]
    mass_weight = mass_weights(size_x, size_y, size_z, weights)
    multiplicity = multiplicities(size_x, size_y, size_z)
    component_creation_rate = reaction_speeds(
        component_share_field,
        scaled_heat_level,
        kinetic_exponents.astype(jnp.float32),
        reaction_change_matrix.astype(jnp.float32),
        logarithm_arrhenius_constant,
        arrhenius_energy_scale,
    )
    expansion_source_field = (
        jnp.einsum(
            "r,retj->etj",
            expansion_contribution_scale,
            component_creation_rate,
            precision=lax.Precision.HIGHEST,
        )
        / scaled_heat_level
    )
    diff_cols = component_spreading_scale[:, None, None, None]
    helm_cols = screened_poisson_reactive_term[:, None, None, None]
    weighted_cond = local_transport_value * mass_weight
    stiff_diag = diag_stiffness(weighted_cond, deriv_mat)
    carried = component_share_field[:species_solved]
    sources = component_creation_rate[:species_solved]
    mass_norm = mass_weight * multiplicity
    stacked = jnp.concatenate(
        [
            (mass_weight * expansion_source_field)[None],
            stiff_diag,
            mass_weight * (helm_cols * carried + sources),
            mass_weight * carried,
        ],
        0,
    )
    summed = fold_rims(padded_2(stacked, ((GX, 1), (GY, 2)), 1))
    div_field = summed[0] / mass_norm
    stiff_sum = summed[1:2]
    rhs = summed[2 : 2 + species_solved] - div_field * summed[2 + species_solved :]
    diag_sum = diff_cols * stiff_sum + helm_cols * mass_norm
    inv_diag = 1.0 / diag_sum
    inv_mult = 1.0 / multiplicity

    def local_dots(first_arr, second_arr):
        return jnp.sum(first_arr * second_arr * inv_mult, axis=(1, 2, 3))

    def operate(values):
        local = (
            diff_cols * stiffness(values, weighted_cond, deriv_mat)
            + helm_cols * mass_weight * values
        )
        return fold_rims(padded_2(local, ((GX, 1), (GY, 2)), 1))

    def paired_sum(first_part, second_part):
        return (over_axes(first_part, GX_GY), over_axes(second_part, GX_GY))

    residual = rhs
    precond_res = inv_diag * residual
    image = operate(precond_res)
    resid_dot, curve_dot = paired_sum(
        local_dots(residual, precond_res), local_dots(image, precond_res)
    )
    step_size = resid_dot / curve_dot
    direction = precond_res
    image_dir = image
    solution = step_size[:, None, None, None] * direction
    residual = residual - step_size[:, None, None, None] * image_dir
    precond_res = inv_diag * residual
    image = operate(precond_res)
    fresh_dot, curve_dot = paired_sum(
        local_dots(residual, precond_res), local_dots(image, precond_res)
    )
    ratio_next = fresh_dot / resid_dot
    step_size = fresh_dot / (curve_dot - ratio_next * fresh_dot / step_size)
    direction = precond_res + ratio_next[:, None, None, None] * direction
    solution = solution + step_size[:, None, None, None] * direction
    return (solution, div_field)


def solution(mesh):
    split = Mesh(mesh.devices.reshape(8, 12, 4, 2), ("gx_0", "gx_1", "gy_0", "gy_1"))
    return jax.shard_map(
        shards,
        mesh=split,
        in_specs=(
            P(None, GX, GY, None),
            P(GX, GY, None),
            P(GX, GY, None),
            P(),
            P(),
            P(),
            P(),
            P(),
            P(),
            P(),
        ),
        out_specs=(P(None, GX, GY, None), P(GX, GY, None)),
        check_vma=False,
    )
```

profile of v0, /device:TPU:1, one launch (start us, length us, event | category | flops | bytes accessed | tf_op | source)
XLA Modules:
  0.0 202.7 jit_solution(16260360397081780304)
XLA Ops:
  0.7 2.0 slice.155
  3.5 4.2 %fusion.1 = f32[128,8192]{1,0:T(8,128)S(1)} fusion(f32[8192]{0:T(1024)S(1)} %bitcast.178, f32[128]{0:T(128)S(1)} %copy-done.15, f32[128]{0:T(128)S(1)} %copy-done.16, f32[4,8,64,128]{3,2,1,0:T(8,128)S(1)} %bitcast.176, s32[128,32]{0,1:T(8,128)S(1)} %copy-done.5), kind=kOutput, calls=%fused_computation.2 | convolution fusion | flops 405803008 | bytes 5293056 | tf_op jit(solution)/shard_map/dot_general | solution.py:124
  7.7 2.5 %fusion.62 = f32[8192,32]{0,1:T(8,128)S(1)} fusion(f32[128,8192]{1,0:T(8,128)S(1)} %fusion.1, s32[32,128]{1,0:T(8,128)S(1)} %copy-done.6), kind=kOutput, calls=%fused_computation.135 | convolution fusion | flops 402657280 | bytes 5259264 | tf_op jit(solution)/shard_map/dot_general | solution.py:129
  16.6 4.8 %collective-permute-start = (f32[34,1,8,128]{3,1,2,0:T(1,128)}, f32[34,1,8,128]{3,1,2,0:T(1,128)S(1)}, u32[]{:S(2)}, u32[]{:S(2)}) collective-permute-start(f32[34,1,8,128]{3,1,2,0:T(1,128)} %get-tuple-element.39), channel_id=1, source_target_pairs={{0,8},{8,16},{16,24},{24,32},{32,40},{40,48},{48,56},{56,64},{64,7... | collective-permute-start | bytes 417800 | tf_op jit(solution)/shard_map/ppermute | solution.py:19
  21.4 15.3 %collective-permute-start.1 = (f32[34,1,8,128]{3,1,2,0:T(1,128)}, f32[34,1,8,128]{3,1,2,0:T(1,128)}, u32[]{:S(2)}, u32[]{:S(2)}) collective-permute-start(f32[34,1,8,128]{3,1,2,0:T(1,128)} %get-tuple-element.40), channel_id=1, source_target_pairs={{8,0},{16,8},{24,16},{32,24},{40,32},{48,40},{56,48},{64,56},{72,6... | collective-permute-start | bytes 417800 | tf_op jit(solution)/shard_map/ppermute | solution.py:22
  40.0 2.6 %collective-permute-start.2 = (f32[34,10,1,128]{3,1,2,0:T(8,128)S(1)}, f32[34,10,1,128]{3,1,2,0:T(8,128)S(1)}, u32[]{:S(2)}, u32[]{:S(2)}) collective-permute-start(f32[34,10,1,128]{3,1,2,0:T(8,128)S(1)} %get-tuple-element.31), channel_id=1, source_target_pairs={{0,1},{1,2},{2,3},{3,4},{4,5},{5,6},{6,7},{7,0},{8,9},{9,10},{10,1... | collective-permute-start | bytes 522248 | tf_op jit(solution)/shard_map/ppermute | solution.py:19
  42.7 3.5 %collective-permute-done.2 = f32[34,10,1,128]{3,1,2,0:T(8,128)S(1)} collective-permute-done((f32[34,10,1,128]{3,1,2,0:T(8,128)S(1)}, f32[34,10,1,128]{3,1,2,0:T(8,128)S(1)}, u32[]{:S(2)}, u32[]{:S(2)}) %collective-permute-start.2) | collective-permute-done | bytes 174112 | tf_op jit(solution)/shard_map/ppermute | solution.py:19
  46.1 2.5 %collective-permute-done.3 = f32[34,10,1,128]{3,1,2,0:T(8,128)S(1)} collective-permute-done((f32[34,10,1,128]{3,1,2,0:T(8,128)S(1)}, f32[34,10,1,128]{3,1,2,0:T(8,128)S(1)}, u32[]{:S(2)}, u32[]{:S(2)}) %collective-permute-start.3) | collective-permute-done | bytes 174112 | tf_op jit(solution)/shard_map/ppermute | solution.py:22
  56.7 1.9 collective-permute-start.4
  58.6 7.4 %collective-permute-start.5 = (f32[16,1,8,128]{3,1,2,0:T(1,128)S(1)}, f32[16,1,8,128]{3,1,2,0:T(1,128)S(1)}, u32[]{:S(2)}, u32[]{:S(2)}) collective-permute-start(f32[16,1,8,128]{3,1,2,0:T(1,128)S(1)} %get-tuple-element.58), channel_id=1, source_target_pairs={{8,0},{16,8},{24,16},{32,24},{40,32},{48,40},{56,48},{64,56},{72,6... | collective-permute-start | bytes 196616 | tf_op jit(solution)/shard_map/ppermute | solution.py:22
  68.5 1.8 collective-permute-done.6
  70.3 2.7 %collective-permute-done.7 = f32[16,10,1,128]{3,1,2,0:T(8,128)S(1)} collective-permute-done((f32[16,10,1,128]{3,1,2,0:T(8,128)S(1)}, f32[16,10,1,128]{3,1,2,0:T(8,128)S(1)}, u32[]{:S(2)}, u32[]{:S(2)}) %collective-permute-start.7) | collective-permute-done | bytes 81952 | tf_op jit(solution)/shard_map/ppermute | solution.py:22
  74.8 10.7 %all-reduce.3 = (f32[16]{0:T(128)S(1)}, f32[16]{0:T(128)S(1)}) all-reduce(f32[16]{0:T(128)S(1)} %get-tuple-element.9, f32[16]{0:T(128)S(1)} %get-tuple-element.8), channel_id=1, replica_groups=mesh['gx_0'=8,'gx_1'=12,'gy_0'=4,'gy_1'=2] {'gx_0'}, use_global_device_ids=true, to_apply=%region_1.2 | all-reduce | flops 32 | bytes 256 | tf_op jit(solution)/shard_map/psum | solution.py:29
  85.5 21.1 %all-reduce.1 = (f32[16]{0:T(128)S(1)}, f32[16]{0:T(128)S(1)}) all-reduce(f32[16]{0:T(128)S(1)} %get-tuple-element.16, f32[16]{0:T(128)S(1)} %get-tuple-element.17), channel_id=1, replica_groups=mesh['gx_0'=8,'gx_1'=12,'gy_0'=4,'gy_1'=2] {'gx_1'}, use_global_device_ids=true, to_apply=%region_2.3 | all-reduce | flops 32 | bytes 256 | tf_op jit(solution)/shard_map/psum | solution.py:29
  106.6 9.9 %all-reduce.5 = (f32[16]{0:T(128)S(1)}, f32[16]{0:T(128)S(1)}) all-reduce(f32[16]{0:T(128)S(1)} %get-tuple-element.12, f32[16]{0:T(128)S(1)} %get-tuple-element.13), channel_id=1, replica_groups=mesh['gx_0'=8,'gx_1'=12,'gy_0'=4,'gy_1'=2] {'gy_0'}, use_global_device_ids=true, to_apply=%region_3.4 | all-reduce | flops 32 | bytes 256 | tf_op jit(solution)/shard_map/psum | solution.py:29
  116.5 10.7 %all-reduce.7 = (f32[16]{0:T(128)S(1)}, f32[16]{0:T(128)S(1)}) all-reduce(f32[16]{0:T(128)S(1)} %get-tuple-element.20, f32[16]{0:T(128)S(1)} %get-tuple-element.21), channel_id=1, replica_groups=mesh['gx_0'=8,'gx_1'=12,'gy_0'=4,'gy_1'=2] {'gy_1'}, use_global_device_ids=true, to_apply=%region_4.5 | all-reduce | flops 32 | bytes 256 | tf_op jit(solution)/shard_map/psum | solution.py:29
  131.3 1.9 collective-permute-start.8
  133.2 6.7 %collective-permute-start.9 = (f32[16,1,8,128]{3,1,2,0:T(1,128)S(1)}, f32[16,1,8,128]{3,1,2,0:T(1,128)S(1)}, u32[]{:S(2)}, u32[]{:S(2)}) collective-permute-start(f32[16,1,8,128]{3,1,2,0:T(1,128)S(1)} %get-tuple-element.52), channel_id=1, source_target_pairs={{8,0},{16,8},{24,16},{32,24},{40,32},{48,40},{56,48},{64,56},{72,6... | collective-permute-start | bytes 196616 | tf_op jit(solution)/shard_map/ppermute | solution.py:22
  141.2 2.9 %collective-permute-start.10 = (f32[16,10,1,128]{3,1,2,0:T(8,128)S(1)}, f32[16,10,1,128]{3,1,2,0:T(8,128)S(1)}, u32[]{:S(2)}, u32[]{:S(2)}) collective-permute-start(f32[16,10,1,128]{3,1,2,0:T(8,128)S(1)} %get-tuple-element.41), channel_id=1, source_target_pairs={{0,1},{1,2},{2,3},{3,4},{4,5},{5,6},{6,7},{7,0},{8,9},{9,10},{10,1... | collective-permute-start | bytes 245768 | tf_op jit(solution)/shard_map/ppermute | solution.py:19
  146.1 2.4 %collective-permute-done.11 = f32[16,10,1,128]{3,1,2,0:T(8,128)S(1)} collective-permute-done((f32[16,10,1,128]{3,1,2,0:T(8,128)S(1)}, f32[16,10,1,128]{3,1,2,0:T(8,128)S(1)}, u32[]{:S(2)}, u32[]{:S(2)}) %collective-permute-start.11) | collective-permute-done | bytes 81952 | tf_op jit(solution)/shard_map/ppermute | solution.py:22
  150.4 11.1 %all-reduce.2 = (f32[16]{0:T(128)S(1)}, f32[16]{0:T(128)S(1)}) all-reduce(f32[16]{0:T(128)S(1)} %get-tuple-element.7, f32[16]{0:T(128)S(1)} %get-tuple-element.6), channel_id=1, replica_groups=mesh['gx_0'=8,'gx_1'=12,'gy_0'=4,'gy_1'=2] {'gx_0'}, use_global_device_ids=true, to_apply=%region_11.12 | all-reduce | flops 32 | bytes 256 | tf_op jit(solution)/shard_map/psum | solution.py:29
  161.5 20.6 %all-reduce = (f32[16]{0:T(128)S(1)}, f32[16]{0:T(128)S(1)}) all-reduce(f32[16]{0:T(128)S(1)} %get-tuple-element.14, f32[16]{0:T(128)S(1)} %get-tuple-element.15), channel_id=1, replica_groups=mesh['gx_0'=8,'gx_1'=12,'gy_0'=4,'gy_1'=2] {'gx_1'}, use_global_device_ids=true, to_apply=%region_12.13 | all-reduce | flops 32 | bytes 256 | tf_op jit(solution)/shard_map/psum | solution.py:29
  182.1 8.6 %all-reduce.4 = (f32[16]{0:T(128)S(1)}, f32[16]{0:T(128)S(1)}) all-reduce(f32[16]{0:T(128)S(1)} %get-tuple-element.10, f32[16]{0:T(128)S(1)} %get-tuple-element.11), channel_id=1, replica_groups=mesh['gx_0'=8,'gx_1'=12,'gy_0'=4,'gy_1'=2] {'gy_0'}, use_global_device_ids=true, to_apply=%region_13.14 | all-reduce | flops 32 | bytes 256 | tf_op jit(solution)/shard_map/psum | solution.py:29
  190.7 10.9 %all-reduce.6 = (f32[16]{0:T(128)S(1)}, f32[16]{0:T(128)S(1)}) all-reduce(f32[16]{0:T(128)S(1)} %get-tuple-element.18, f32[16]{0:T(128)S(1)} %get-tuple-element.19), channel_id=1, replica_groups=mesh['gx_0'=8,'gx_1'=12,'gy_0'=4,'gy_1'=2] {'gy_1'}, use_global_device_ids=true, to_apply=%region_14.15 | all-reduce | flops 32 | bytes 256 | tf_op jit(solution)/shard_map/psum | solution.py:29
  (115 shorter events, 32.7 us)
Async XLA Ops:
  0.6 10.7 %copy-start = (f32[32]{0:T(128)S(1)}, f32[32]{0:T(128)}, u32[]{:S(2)}) copy-start(f32[32]{0:T(128)} %param.18) | copy-start | bytes 388
  0.6 2.0 copy-start.1
  0.7 2.2 %copy-start.11 = (f32[8]{0:T(128)S(1)}, f32[8]{0:T(128)}, u32[]{:S(2)}) copy-start(f32[8]{0:T(128)} %constant.68.clone) | copy-start | bytes 100
  2.7 0.8 copy-start.15
  3.5 4.2 %copy-start.6 = (s32[32,128]{1,0:T(8,128)S(1)}, s32[32,128]{1,0:T(8,128)}, u32[]{:S(2)}) copy-start(s32[32,128]{1,0:T(8,128)} %param.22) | copy-start | bytes 49156
  11.1 1.5 copy-start.4
  11.1 1.6 copy-start.7
  11.1 1.9 copy-start.12
  11.1 1.9 copy-start.13
  11.1 1.9 copy-start.14
  13.0 1.2 copy-start.8
  16.6 21.6 %collective-permute-start = (f32[34,1,8,128]{3,1,2,0:T(1,128)}, f32[34,1,8,128]{3,1,2,0:T(1,128)S(1)}, u32[]{:S(2)}, u32[]{:S(2)}) collective-permute-start(f32[34,1,8,128]{3,1,2,0:T(1,128)} %get-tuple-element.39), channel_id=1, source_target_pairs={{0,8},{8,16},{16,24},{24,32},{32,40},{40,48},{48,56},{56,64},{64,7... | collective-permute-start | bytes 417800 | tf_op jit(solution)/shard_map/ppermute | solution.py:19
  21.4 17.8 %collective-permute-start.1 = (f32[34,1,8,128]{3,1,2,0:T(1,128)}, f32[34,1,8,128]{3,1,2,0:T(1,128)}, u32[]{:S(2)}, u32[]{:S(2)}) collective-permute-start(f32[34,1,8,128]{3,1,2,0:T(1,128)} %get-tuple-element.40), channel_id=1, source_target_pairs={{8,0},{16,8},{24,16},{32,24},{40,32},{48,40},{56,48},{64,56},{72,6... | collective-permute-start | bytes 417800 | tf_op jit(solution)/shard_map/ppermute | solution.py:22
  40.0 6.1 %collective-permute-start.2 = (f32[34,10,1,128]{3,1,2,0:T(8,128)S(1)}, f32[34,10,1,128]{3,1,2,0:T(8,128)S(1)}, u32[]{:S(2)}, u32[]{:S(2)}) collective-permute-start(f32[34,10,1,128]{3,1,2,0:T(8,128)S(1)} %get-tuple-element.31), channel_id=1, source_target_pairs={{0,1},{1,2},{2,3},{3,4},{4,5},{5,6},{6,7},{7,0},{8,9},{9,10},{10,1... | collective-permute-start | bytes 522248 | tf_op jit(solution)/shard_map/ppermute | solution.py:19
  42.6 6.0 %collective-permute-start.3 = (f32[34,10,1,128]{3,1,2,0:T(8,128)S(1)}, f32[34,10,1,128]{3,1,2,0:T(8,128)S(1)}, u32[]{:S(2)}, u32[]{:S(2)}) collective-permute-start(f32[34,10,1,128]{3,1,2,0:T(8,128)S(1)} %get-tuple-element.32), channel_id=1, source_target_pairs={{1,0},{2,1},{3,2},{4,3},{5,4},{6,5},{7,6},{0,7},{9,8},{10,9},{11,1... | collective-permute-start | bytes 522248 | tf_op jit(solution)/shard_map/ppermute | solution.py:22
  51.5 0.9 copy-start.9
  56.7 9.8 %collective-permute-start.4 = (f32[16,1,8,128]{3,1,2,0:T(1,128)S(1)}, f32[16,1,8,128]{3,1,2,0:T(1,128)S(1)}, u32[]{:S(2)}, u32[]{:S(2)}) collective-permute-start(f32[16,1,8,128]{3,1,2,0:T(1,128)S(1)} %get-tuple-element.57), channel_id=1, source_target_pairs={{0,8},{8,16},{16,24},{24,32},{32,40},{40,48},{48,56},{56,64},{64,7... | collective-permute-start | bytes 196616 | tf_op jit(solution)/shard_map/ppermute | solution.py:19
  58.6 8.8 %collective-permute-start.5 = (f32[16,1,8,128]{3,1,2,0:T(1,128)S(1)}, f32[16,1,8,128]{3,1,2,0:T(1,128)S(1)}, u32[]{:S(2)}, u32[]{:S(2)}) collective-permute-start(f32[16,1,8,128]{3,1,2,0:T(1,128)S(1)} %get-tuple-element.58), channel_id=1, source_target_pairs={{8,0},{16,8},{24,16},{32,24},{40,32},{48,40},{56,48},{64,56},{72,6... | collective-permute-start | bytes 196616 | tf_op jit(solution)/shard_map/ppermute | solution.py:22
  67.4 2.8 %collective-permute-start.6 = (f32[16,10,1,128]{3,1,2,0:T(8,128)S(1)}, f32[16,10,1,128]{3,1,2,0:T(8,128)S(1)}, u32[]{:S(2)}, u32[]{:S(2)}) collective-permute-start(f32[16,10,1,128]{3,1,2,0:T(8,128)S(1)} %get-tuple-element.43), channel_id=1, source_target_pairs={{0,1},{1,2},{2,3},{3,4},{4,5},{5,6},{6,7},{7,0},{8,9},{9,10},{10,1... | collective-permute-start | bytes 245768 | tf_op jit(solution)/shard_map/ppermute | solution.py:19
  68.3 4.7 %collective-permute-start.7 = (f32[16,10,1,128]{3,1,2,0:T(8,128)S(1)}, f32[16,10,1,128]{3,1,2,0:T(8,128)S(1)}, u32[]{:S(2)}, u32[]{:S(2)}) collective-permute-start(f32[16,10,1,128]{3,1,2,0:T(8,128)S(1)} %get-tuple-element.44), channel_id=1, source_target_pairs={{1,0},{2,1},{3,2},{4,3},{5,4},{6,5},{7,6},{0,7},{9,8},{10,9},{11,1... | collective-permute-start | bytes 245768 | tf_op jit(solution)/shard_map/ppermute | solution.py:22
  131.3 8.6 %collective-permute-start.8 = (f32[16,1,8,128]{3,1,2,0:T(1,128)S(1)}, f32[16,1,8,128]{3,1,2,0:T(1,128)S(1)}, u32[]{:S(2)}, u32[]{:S(2)}) collective-permute-start(f32[16,1,8,128]{3,1,2,0:T(1,128)S(1)} %get-tuple-element.51), channel_id=1, source_target_pairs={{0,8},{8,16},{16,24},{24,32},{32,40},{40,48},{48,56},{56,64},{64,7... | collective-permute-start | bytes 196616 | tf_op jit(solution)/shard_map/ppermute | solution.py:19
  133.2 8.0 %collective-permute-start.9 = (f32[16,1,8,128]{3,1,2,0:T(1,128)S(1)}, f32[16,1,8,128]{3,1,2,0:T(1,128)S(1)}, u32[]{:S(2)}, u32[]{:S(2)}) collective-permute-start(f32[16,1,8,128]{3,1,2,0:T(1,128)S(1)} %get-tuple-element.52), channel_id=1, source_target_pairs={{8,0},{16,8},{24,16},{32,24},{40,32},{48,40},{56,48},{64,56},{72,6... | collective-permute-start | bytes 196616 | tf_op jit(solution)/shard_map/ppermute | solution.py:22
  141.2 4.8 %collective-permute-start.10 = (f32[16,10,1,128]{3,1,2,0:T(8,128)S(1)}, f32[16,10,1,128]{3,1,2,0:T(8,128)S(1)}, u32[]{:S(2)}, u32[]{:S(2)}) collective-permute-start(f32[16,10,1,128]{3,1,2,0:T(8,128)S(1)} %get-tuple-element.41), channel_id=1, source_target_pairs={{0,1},{1,2},{2,3},{3,4},{4,5},{5,6},{6,7},{7,0},{8,9},{9,10},{10,1... | collective-permute-start | bytes 245768 | tf_op jit(solution)/shard_map/ppermute | solution.py:19
  144.2 4.4 %collective-permute-start.11 = (f32[16,10,1,128]{3,1,2,0:T(8,128)S(1)}, f32[16,10,1,128]{3,1,2,0:T(8,128)S(1)}, u32[]{:S(2)}, u32[]{:S(2)}) collective-permute-start(f32[16,10,1,128]{3,1,2,0:T(8,128)S(1)} %get-tuple-element.42), channel_id=1, source_target_pairs={{1,0},{2,1},{3,2},{4,3},{5,4},{6,5},{7,6},{0,7},{9,8},{10,9},{11,1... | collective-permute-start | bytes 245768 | tf_op jit(solution)/shard_map/ppermute | solution.py:22
  (5 other events, 3.7 us)
where the time goes:
time: 203 us
  blocking collectives  104 us (51%)
  starting transfers between devices  44.6 us (22%)
  waiting for transfers between devices  18.2 us (9%)
  matrix products  15.9 us (8%)
  other arithmetic  10.1 us (5%)
  local copies, waits for them, and re-layouts  9.04 us (4%)
    psum x8, blocking collectives, over_axes(): array = lax.psum(array, axis)  104 us
    ppermute x6, starting transfers between devices, padded_2(): lax.ppermute(lax.slice_in_dim(block, 0, width, axis=dim), axis, backward)  29.6 us
    ppermute x6, starting transfers between devices, padded_2(): lax.ppermute(lax.slice_in_dim(block, block.shape[dim] - width, None, axis...  15 us
    ppermute x6, waiting for transfers between devices, padded_2(): lax.ppermute(lax.slice_in_dim(block, 0, width, axis=dim), axis, backward)  10.9 us
    ppermute x6, waiting for transfers between devices, padded_2(): lax.ppermute(lax.slice_in_dim(block, block.shape[dim] - width, None, axis...  7.37 us
    dot_general x1, matrix products, reaction_speeds(): jnp.dot(kinetic_exponents_float, log_frac, precision=lax.Precision.HIGHEST)  4.15 us
  transfers between devices with their start and end apart: 12, of which 11 were waited for; matrix products, arithmetic and copies ran while one was open for 1% of the time, Pallas kernels for 0%

commit v1 on v0

v1 whole, which is shorter than its diff:
```python
import functools

import jax
import jax.numpy as jnp
import numpy as np
from jax import lax
from jax.experimental import pallas as pl
from jax.experimental.pallas import tpu as pltpu
from jax.sharding import PartitionSpec as P

MESH = pl.DeviceIdType.MESH
F32 = jnp.float32
BF16 = jnp.bfloat16
NZ = 12
XY = 64
NS = 16
DIRS = ((-1, 0), (1, 0), (0, -1), (0, 1), (-1, -1), (-1, 1), (1, -1), (1, 1))
OPPOSITE = (1, 0, 3, 2, 7, 6, 5, 4)
SPOTS = (
    [p for p in range(8)],
    [56 + p for p in range(8)],
    [8 * p for p in range(8)],
    [8 * p + 7 for p in range(8)],
    [0],
    [7],
    [56],
    [63],
)


def legendre_seven(points):
    return (429.0 * points**7 - 693.0 * points**5 + 315.0 * points**3 - 35.0 * points) / 16.0


def gll_tables():
    gll_nodes = np.array(
        [
            -1.0,
            -0.8717401485096066,
            -0.5917001814331423,
            -0.2092992179024789,
            0.2092992179024789,
            0.5917001814331423,
            0.8717401485096066,
            1.0,
        ]
    )
    at_nodes = legendre_seven(gll_nodes)
    weights = 2.0 / (56.0 * at_nodes * at_nodes)
    derivative = np.zeros((8, 8))
    for row_index in range(8):
        for col_index in range(8):
            if row_index != col_index:
                derivative[row_index, col_index] = at_nodes[row_index] / (
                    at_nodes[col_index] * (gll_nodes[row_index] - gll_nodes[col_index])
                )
    derivative[0, 0] = -14.0
    derivative[7, 7] = 14.0
    return (derivative, weights)


def constant_table():
    derivative, weights = gll_tables()
    d32 = derivative.astype(np.float32)
    w32 = weights.astype(np.float32)
    square = d32 * d32
    eye8 = np.eye(8, dtype=np.float32)
    eye16 = np.eye(16, dtype=np.float32)
    along_z = np.kron(eye16, d32)
    plane = np.kron(square.T, eye8) + np.kron(eye8, square.T)
    mass = (w32[:, None, None] * w32[None, :, None]) * np.tile(w32, 16)[None, None, :]
    ends = np.array([2.0, 1, 1, 1, 1, 1, 1, 2.0], np.float32)
    mult = (ends[:, None, None] * ends[None, :, None]) * np.tile(ends, 16)[None, None, :]
    return np.concatenate(
        [
            along_z.T,
            along_z,
            np.kron(eye16, square),
            np.pad(plane, ((0, 0), (0, 64))),
            mass.reshape(64, 128),
            mult.reshape(64, 128),
        ],
        0,
    ).astype(np.float32)


def half_matrices(matrix):
    flipped = matrix[:4, ::-1][:, :4]
    even = 0.5 * (matrix[:4, :4] + flipped)
    odd = 0.5 * (matrix[:4, :4] - flipped)
    return [[float(np.float32(v)) for v in row] for row in even], [
        [float(np.float32(v)) for v in row] for row in odd
    ]


FORWARD = half_matrices(gll_tables()[0])
BACKWARD = half_matrices(gll_tables()[0].T)


def apply_line(values, halves):
    even_mat, odd_mat = halves
    even = [values[j] + values[7 - j] for j in range(4)]
    odd = [values[j] - values[7 - j] for j in range(4)]
    low, high = [], []
    for i in range(4):
        first = even_mat[i][0] * even[0]
        second = odd_mat[i][0] * odd[0]
        for j in range(1, 4):
            first = first + even_mat[i][j] * even[j]
            second = second + odd_mat[i][j] * odd[j]
        low.append(second + first)
        high.append(second - first)
    return low + high[::-1]


def stiff_line(values, weights):
    slopes = apply_line(values, FORWARD)
    return apply_line([s * w for s, w in zip(slopes, weights)], BACKWARD)


def pieces(value):
    first = value.astype(BF16)
    rest = value - first.astype(F32)
    second = rest.astype(BF16)
    third = (rest - second.astype(F32)).astype(BF16)
    return first, second, third


def kernel(nz, ny, ng, *refs):
    ins, outs, rest = refs[:11], refs[11:13], refs[13:]
    loads, rest = rest[:11], rest[11:]
    (
        ee_ref,
        cc_ref,
        g_ref,
        wrow_ref,
        diag_ref,
        div_ref,
        my_ref,
        mp_ref,
        wb_ref,
        hm_ref,
        inv_ref,
        z_ref,
        v_ref,
        y_ref,
        sface,
        scorn,
        rface,
        rcorn,
        srow,
        rrow,
        load_sem,
        send_sem,
        recv_sem,
        row_send,
        row_recv,
    ) = rest
    share, heat, cond, diff1, helm1, expn1, loga1, ea1, kin, chg, table = loads
    out_ref, divout_ref = outs

    gx = lax.axis_index("gx")
    gy = lax.axis_index("gy")
    at_y = lax.div(gx, nz)
    at_z = lax.rem(gx, nz)
    nx = nz * ny

    def neighbour(d):
        sx, sy = DIRS[d]
        return (lax.rem(gx + (sx + nx), nx), lax.rem(gy + (sy + ng), ng))

    def peer_g(k):
        return (gx, lax.rem(gy + k, ng))

    def peer_y(k):
        return (lax.rem(at_y + k, ny) * nz + at_z, gy)

    def peer_z(k):
        return (at_y * nz + lax.rem(at_z + k, nz), gy)

    barrier = pltpu.get_barrier_semaphore()
    greeted = [neighbour(d) for d in range(8)]
    greeted += [peer_g(k) for k in range(1, ng)]
    greeted += [peer_y(k) for k in range(1, ny)]
    greeted += [peer_z(k) for k in range(1, nz)]

    fetch = [pltpu.make_async_copy(ins[i], loads[i], load_sem.at[i]) for i in range(11)]
    for one in fetch:
        one.start()
    for device in greeted:
        pl.semaphore_signal(barrier, inc=1, device_id=device, device_id_type=MESH)
    for one in fetch:
        one.wait()

    lane = lax.broadcasted_iota(jnp.int32, (NS, 128), 1)
    sub = lax.broadcasted_iota(jnp.int32, (NS, 128), 0)
    node = lane & 7
    first_node = node == 0
    last_node = node == 7

    def column(row, rows):
        at_lane = lax.broadcasted_iota(jnp.int32, (rows, row.shape[1]), 1)
        at_sub = lax.broadcasted_iota(jnp.int32, (rows, row.shape[1]), 0)
        spread = jnp.broadcast_to(row, (rows, row.shape[1]))
        return jnp.sum(jnp.where(at_lane == at_sub, spread, 0.0), axis=1, keepdims=True)

    def zsum(value):
        before = pltpu.roll(value, 1, 1)
        after = pltpu.roll(value, 127, 1)
        count = value.shape[0]
        return value + jnp.where(
            first_node[:count], before, jnp.where(last_node[:count], after, 0.0)
        )

    diff = jnp.broadcast_to(column(diff1[...], NS), (NS, 128))
    helm = jnp.broadcast_to(column(helm1[...], NS), (NS, 128))

    ea = column(ea1[...], 128)
    const = column(loga1[...], 128) + ea
    ee_ref[...] = jnp.zeros((128, 128), F32)
    ee_ref[:, 0:32] = kin[...].astype(F32)
    base = ee_ref[...]
    base = base + pltpu.roll(base, 32, 1) + pltpu.roll(base, 64, 1)
    ea_p = [p.astype(F32) for p in pieces(-ea)]
    co_p = [p.astype(F32) for p in pieces(const)]
    lane128 = lax.broadcasted_iota(jnp.int32, (128, 128), 1)
    extra = [ea_p[0], ea_p[0], ea_p[0], ea_p[1], ea_p[1], ea_p[2], co_p[0], co_p[1], co_p[2]]
    for i, col in enumerate(extra):
        base = jnp.where(lane128 == 96 + i, col, base)
    ee_ref[...] = base
    change = chg[...].astype(F32)
    weighted = jnp.sum(column(expn1[...], 32) * change, axis=0, keepdims=True)
    we_p = [p.astype(F32) for p in pieces(weighted)]
    sub16 = lax.broadcasted_iota(jnp.int32, (NS, 128), 0)
    tail = jnp.where(
        sub16 == 0,
        we_p[0],
        jnp.where(sub16 == 1, we_p[1], jnp.where(sub16 == 2, we_p[2], 0.0)),
    )
    cc_ref[0:16, :] = change[:16]
    cc_ref[16:32, :] = tail

    inverse = 1.0 / heat[...]
    in_p = pieces(inverse)
    for i in range(3):
        g_ref[i] = in_p[i].astype(F32)
    g_ref[3] = inverse * table[448:512, :]

    wrow_ref[...] = cond[...] * table[448:512, :]
    diag_ref[...] = jnp.dot(
        table[384:448, 0:64], wrow_ref[...], precision=lax.Precision.HIGHEST, preferred_element_type=F32
    ) + jnp.dot(
        wrow_ref[...], table[256:384, :], precision=lax.Precision.HIGHEST, preferred_element_type=F32
    )

    def spread_rows(at, carry):
        mass = jnp.broadcast_to(table[pl.ds(448 + at, 1), :], (NS, 128))
        wb_ref[at] = jnp.broadcast_to(wrow_ref[pl.ds(at, 1), :], (NS, 128))
        hm_ref[at] = helm * mass
        my_ref[at] = mass * share[pl.ds(at, NS, stride=XY), :]
        return carry

    lax.fori_loop(0, XY, spread_rows, 0)

    def chem(first):
        logs, gparts = [], []
        for j in range(4):
            logs.append(jnp.log(share[pl.ds(first + j, 32, stride=XY), :]))
            rows = [jnp.broadcast_to(g_ref[i, pl.ds(first + j, 1), :], (NS, 128)) for i in range(3)]
            one = jnp.where(
                (sub == 0) | (sub == 3) | (sub == 5),
                rows[0],
                jnp.where((sub == 1) | (sub == 4), rows[1], jnp.where(sub == 2, rows[2], 1.0)),
            )
            gparts.append(one)
        log_p = pieces(jnp.concatenate(logs, axis=1))
        gpart = jnp.concatenate(gparts, axis=1).astype(BF16)
        stacked = jnp.concatenate([*log_p, gpart, gpart], axis=0)
        exponent = jnp.dot(ee_ref[...].astype(BF16), stacked, preferred_element_type=F32)
        prog = jnp.concatenate(pieces(jnp.exp(exponent)), axis=0)
        made = cc_ref[...].astype(BF16)
        made = jnp.dot(jnp.concatenate([made, made, made], axis=1), prog, preferred_element_type=F32)
        for j in range(4):
            at = first + j
            part = made[:, 128 * j : 128 * (j + 1)]
            mp_ref[at] = table[pl.ds(448 + at, 1), :] * part[:NS]
            total = part[16:17] + part[17:18] + part[18:19]
            div_ref[pl.ds(at, 1), :] = total * g_ref[3, pl.ds(at, 1), :]

    def chem_ends(i, carry):
        chem(4 * i + 48 * lax.div(i, 2))
        return carry

    def chem_mid(i, carry):
        chem(8 + 4 * i)
        return carry

    def pack(stage, d, field, scalar):
        spots = SPOTS[d]
        if d < 4:
            for p, at in enumerate(spots):
                sface[stage, d, 16 * p : 16 * p + 16, :] = field[at]
            if scalar is not None:
                sface[stage, d, 128:136, :] = scalar[pl.ds(spots[0], 8, stride=spots[1] - spots[0]), :]
        else:
            at = spots[0]
            scorn[stage, d - 4, 0:16, :] = field[at]
            if scalar is not None:
                scorn[stage, d - 4, 16:24, :] = jnp.broadcast_to(scalar[at : at + 1, :], (8, 128))

    def transfer(stage, d):
        if d < 4:
            source, target = sface.at[stage, d], rface.at[stage, d]
            if stage == 2:
                source, target = source.at[0:128], target.at[0:128]
        else:
            source, target = scorn.at[stage, d - 4], rcorn.at[stage, d - 4]
            if stage == 2:
                source, target = source.at[0:16], target.at[0:16]
        return pltpu.make_async_remote_copy(
            src_ref=source,
            dst_ref=target,
            send_sem=send_sem.at[8 * stage + d],
            recv_sem=recv_sem.at[8 * stage + d],
            device_id=neighbour(d),
            device_id_type=MESH,
        )

    def unpack(stage, d, field, scalar):
        spots = SPOTS[OPPOSITE[d]]
        if d < 4:
            for p, at in enumerate(spots):
                field[at] = field[at] + rface[stage, d, 16 * p : 16 * p + 16, :]
            if scalar is not None:
                where = pl.ds(spots[0], 8, stride=spots[1] - spots[0])
                scalar[where, :] = scalar[where, :] + rface[stage, d, 128:136, :]
        else:
            at = spots[0]
            field[at] = field[at] + rcorn[stage, d - 4, 0:16, :]
            if scalar is not None:
                scalar[at : at + 1, :] = scalar[at : at + 1, :] + rcorn[stage, d - 4, 16:17, :]

    sent = []

    def send(stage, d, field, scalar):
        pack(stage, d, field, scalar)
        copy = transfer(stage, d)
        copy.start()
        sent.append((stage, d, copy))

    def collect(stage, field, scalar):
        for at_stage, d, copy in sent:
            if at_stage == stage:
                copy.wait_recv()
                unpack(stage, d, field, scalar)

    lax.fori_loop(0, 4, chem_ends, 0)
    pl.semaphore_wait(barrier, len(greeted))
    for d in range(8):
        send(0, d, my_ref, diag_ref)
    for d in (0, 1, 4, 5, 6, 7):
        send(1, d, mp_ref, div_ref)
    lax.fori_loop(0, 12, chem_mid, 0)
    for d in (2, 3):
        send(1, d, mp_ref, div_ref)

    collect(0, my_ref, diag_ref)
    for x in range(8):
        diag_ref[8 * x : 8 * x + 8, :] = zsum(diag_ref[8 * x : 8 * x + 8, :])

    def invert(at, carry):
        total = diff * diag_ref[pl.ds(at, 1), :] + hm_ref[at] * table[pl.ds(512 + at, 1), :]
        inv_ref[at] = 1.0 / total
        return carry

    lax.fori_loop(0, XY, invert, 0)

    collect(1, mp_ref, div_ref)
    for x in range(8):
        here = slice(8 * x, 8 * x + 8)
        norm = table[448 + 8 * x : 456 + 8 * x, :] * table[512 + 8 * x : 520 + 8 * x, :]
        field = zsum(div_ref[here, :]) / norm
        div_ref[here, :] = field
        divout_ref[here, :] = field

    none = jnp.zeros((NS, 128), F32)

    def share_of(at):
        return 1.0 / table[pl.ds(512 + at, 1), :]

    def start(at, acc):
        local = mp_ref[at] + (helm - div_ref[pl.ds(at, 1), :]) * my_ref[at]
        resid = zsum(local)
        precond = inv_ref[at] * resid
        z_ref[at] = precond
        return acc + resid * precond * share_of(at)

    dot_a = lax.fori_loop(0, XY, start, none)

    def operate(source):
        def z_part(x, carry):
            here = pl.ds(8 * x, 8)
            value = source[here].reshape(128, 128)
            slope = jnp.dot(
                value, table[0:128, :], precision=lax.Precision.HIGHEST, preferred_element_type=F32
            )
            slope = slope * wb_ref[here].reshape(128, 128)
            back = jnp.dot(
                slope, table[128:256, :], precision=lax.Precision.HIGHEST, preferred_element_type=F32
            )
            y_ref[here] = back.reshape(8, NS, 128)
            return carry

        def x_part(y, carry):
            got = stiff_line([source[8 * x + y] for x in range(8)], [wb_ref[8 * x + y] for x in range(8)])
            for x in range(8):
                y_ref[8 * x + y] = y_ref[8 * x + y] + got[x]
            return carry

        def y_part(x, acc):
            values = [source[8 * x + y] for y in range(8)]
            got = stiff_line(values, [wb_ref[8 * x + y] for y in range(8)])
            for y in range(8):
                at = 8 * x + y
                image = diff * (y_ref[at] + got[y]) + hm_ref[at] * values[y]
                y_ref[at] = image
                acc = acc + values[y] * image
            return acc

        lax.fori_loop(0, 8, z_part, 0)
        lax.fori_loop(0, 8, x_part, 0)
        return lax.fori_loop(0, 8, y_part, none)

    dot_c = operate(z_ref)
    for d in range(8):
        send(2, d, y_ref, None)
    collect(2, y_ref, None)

    def second(at, acc):
        image = zsum(y_ref[at])
        precond = inv_ref[at] * image
        v_ref[at] = precond
        return acc + image * precond * share_of(at)

    dot_b = lax.fori_loop(0, XY, second, none)
    dot_d = operate(v_ref)

    packed = none
    for q, acc in enumerate((dot_a, dot_c, dot_b, dot_d)):
        packed = packed + jnp.where(lane == 16 * q + sub, jnp.sum(acc, axis=1, keepdims=True), 0.0)
    row = jnp.sum(packed, axis=0, keepdims=True)

    rows_sent = []
    slot = 0
    for phase, (count, peer) in enumerate(((ng, peer_g), (ny, peer_y), (nz, peer_z))):
        srow[phase] = row
        copies = []
        for k in range(1, count):
            copy = pltpu.make_async_remote_copy(
                src_ref=srow.at[phase],
                dst_ref=rrow.at[slot],
                send_sem=row_send.at[slot],
                recv_sem=row_recv.at[slot],
                device_id=peer(k),
                device_id_type=MESH,
            )
            copy.start()
            copies.append((slot, copy))
            slot += 1
        for _, copy in copies:
            copy.wait_recv()
        for at, _ in copies:
            row = row + rrow[at]
        rows_sent += [copy for _, copy in copies]

    totals = jnp.broadcast_to(row, (NS, 128))
    a, c, b, d = [
        jnp.sum(jnp.where(lane == 16 * q + sub, totals, 0.0), axis=1, keepdims=True) for q in range(4)
    ]
    ratio = b / c
    gamma = (c - ratio * a) / (d - ratio * b)
    alpha = a / c - gamma * ratio
    alpha = jnp.broadcast_to(alpha, (NS, 128))
    gamma = jnp.broadcast_to(gamma, (NS, 128))

    def finish(at, carry):
        out_ref[pl.ds(at, NS, stride=XY), :] = alpha * z_ref[at] + gamma * v_ref[at]
        return carry

    lax.fori_loop(0, XY, finish, 0)

    for _, _, copy in sent:
        copy.wait_send()
    for copy in rows_sent:
        copy.wait_send()


def shards(nz, ny, ng, *args):
    share, heat, cond, diff, helm, expn, loga, ea, kin, chg = args
    count = (ng - 1) + (ny - 1) + (nz - 1)
    operands = [
        share.reshape(32 * XY, 128),
        heat.reshape(XY, 128),
        cond.reshape(XY, 128),
        diff.reshape(1, NS),
        helm.reshape(1, NS),
        expn.reshape(1, 32),
        loga.reshape(1, 128),
        ea.reshape(1, 128),
        kin,
        chg,
        jnp.asarray(constant_table()),
    ]
    cube = pltpu.VMEM((XY, NS, 128), F32)
    out, div = pl.pallas_call(
        functools.partial(kernel, nz, ny, ng),
        out_shape=(
            jax.ShapeDtypeStruct((NS * XY, 128), F32),
            jax.ShapeDtypeStruct((XY, 128), F32),
        ),
        in_specs=[pl.BlockSpec(memory_space=pl.ANY)] * 11,
        out_specs=(
            pl.BlockSpec(memory_space=pltpu.VMEM),
            pl.BlockSpec(memory_space=pltpu.VMEM),
        ),
        scratch_shapes=[pltpu.VMEM(o.shape, o.dtype) for o in operands]
        + [
            pltpu.VMEM((128, 128), F32),
            pltpu.VMEM((32, 128), F32),
            pltpu.VMEM((4, XY, 128), F32),
            pltpu.VMEM((XY, 128), F32),
            pltpu.VMEM((XY, 128), F32),
            pltpu.VMEM((XY, 128), F32),
        ]
        + [cube] * 8
        + [
            pltpu.VMEM((3, 4, 136, 128), F32),
            pltpu.VMEM((3, 4, 24, 128), F32),
            pltpu.VMEM((3, 4, 136, 128), F32),
            pltpu.VMEM((3, 4, 24, 128), F32),
            pltpu.VMEM((3, 1, 128), F32),
            pltpu.VMEM((count, 1, 128), F32),
            pltpu.SemaphoreType.DMA((11,)),
            pltpu.SemaphoreType.DMA((24,)),
            pltpu.SemaphoreType.DMA((24,)),
            pltpu.SemaphoreType.DMA((count,)),
            pltpu.SemaphoreType.DMA((count,)),
        ],
        compiler_params=pltpu.CompilerParams(
            collective_id=0, has_side_effects=True, vmem_limit_bytes=40 * 1024 * 1024
        ),
        name="reacting_step",
    )(*operands)
    return out.reshape(NS, 8, 8, 128), div.reshape(8, 8, 128)


def solution(mesh):
    ng = mesh.shape["gy"]
    ny = mesh.shape["gx"] // NZ
    field = P("gx", "gy", None)
    species = P(None, "gx", "gy", None)
    return jax.shard_map(
        functools.partial(shards, NZ, ny, ng),
        mesh=mesh,
        in_specs=(species, field, field, P(), P(), P(), P(), P(), P(), P()),
        out_specs=(species, field),
        check_vma=False,
    )
```

time: 203 us -> 71.8 us (0.35)
  blocking collectives: 104 us -> 0 us
  Pallas kernels: 0 us -> 65.8 us
  starting transfers between devices: 44.6 us -> 0 us
  waiting for transfers between devices: 18.2 us -> 0 us
  matrix products: 15.9 us -> 0 us
  other arithmetic: 10.1 us -> 0 us
  local copies, waits for them, and re-layouts: 9.04 us -> 4.48 us
    psum x8 -> x0, blocking collectives: 104 us -> none  [over_axes(): array = lax.psum(array, axis)]
    pallas_call x0 -> x1, Pallas kernels: none -> 65.8 us  [shards(): pl.pallas_call(functools.partial(kernel, nz, ny, ng), out_shape=(jax.Shap...]
    ppermute x12 -> x0, starting transfers between devices: 44.6 us -> none  [the longest x6 29.6 us: padded_2(): lax.ppermute(lax.slice_in_dim(block, 0, width, axis=dim), axis, backward)]
    ppermute x12 -> x0, waiting for transfers between devices: 18.2 us -> none  [the longest x6 10.9 us: padded_2(): lax.ppermute(lax.slice_in_dim(block, 0, width, axis=dim), axis, backward)]
    dot_general x18 -> x0, matrix products: 15.9 us -> none  [the longest x1 4.15 us: reaction_speeds(): jnp.dot(kinetic_exponents_float, log_frac, precision=lax.Precision.HIGHEST)]
    slice x9 -> x0, local copies, waits for them, and re-layouts: 3.8 us -> none  [the longest x1 1.98 us: shards(): carried = component_share_field[:species_solved]]
    mul x6 -> x0, other arithmetic: 2.42 us -> none  [the longest x1 1.44 us: shards(): mass_weight * (helm_cols * carried + sources)]
    add x8 -> x0, other arithmetic: 2.28 us -> none  [the longest x3 0.85 us: fold_rims(): padded[:, 1:-1] + jnp.where(low_x, padded[:, :-2], 0.0)]
  transfers between devices with their start and end apart: 12 -> 0, of which waited for: 11 -> 0; matrix products, arithmetic and copies ran while one was open for 1% -> 0% of each run, Pallas kernels for 0% -> 0%
where the time goes in v1:
time: 71.8 us; the launch traced here: 71.1 us
  Pallas kernels  65.8 us (92%)
  local copies, waits for them, and re-layouts  4.48 us (6%)
  between operations  0.78 us (1%)
    pallas_call x1, Pallas kernels, shards(): pl.pallas_call(functools.partial(kernel, nz, ny, ng), out_shape=(jax.Shap...  65.8 us
    unnamed x23, local copies, waits for them, and re-layouts  4.48 us

profile of v1, /device:TPU:1, one launch (start us, length us, event | category | flops | bytes accessed | tf_op | source)
XLA Modules:
  0.0 71.1 jit_solution(298639155003940240)
XLA Ops:
  0.6 0.0 copy-start.8
  0.6 0.0 copy-start.9
  0.7 0.0 copy-start.5
  0.7 0.0 copy-start.6
  0.7 0.0 copy-start.7
  0.7 0.0 copy-start.2
  0.7 0.0 copy-start.3
  0.7 0.0 copy-start.4
  0.7 0.9 %copy.13.refs_8_ = s32[128,32]{1,0:T(8,128)S(1)} copy(s32[128,32]{0,1:T(8,128)} %param.19) | data formatting | bytes 32768 | tf_op args[8]
  1.6 0.0 copy-done.8
  1.6 0.0 copy-done.9
  1.6 0.0 copy-done.5
  1.6 0.0 copy-done.6
  1.6 0.0 copy-done.7
  1.6 0.0 copy-done.2
  1.6 0.0 copy-done.3
  1.6 0.0 copy-done.4
  1.7 0.0 copy-start
  1.7 1.2 %copy-done = f32[32,8,8,128]{3,2,1,0:T(8,128)S(1)} copy-done((f32[32,8,8,128]{3,2,1,0:T(8,128)S(1)}, f32[32,8,8,128]{3,2,1,0:T(8,128)}, u32[]{:S(2)}) %copy-start) | copy-done | bytes 1048600
  2.9 0.0 copy-start.1
  2.9 1.0 %copy-done.1 = f32[576,128]{1,0:T(8,128)S(1)} copy-done((f32[576,128]{1,0:T(8,128)S(1)}, f32[576,128]{1,0:T(8,128)}, u32[]{:S(2)}) %copy-start.1) | copy-done | bytes 294936
  3.8 65.8 %reacting_step.1 = (f32[1024,128]{1,0:T(8,128)S(1)}, f32[64,128]{1,0:T(8,128)S(1)}) custom-call(f32[2048,128]{1,0:T(8,128)S(1)} %bitcast.10, f32[64,128]{1,0:T(8,128)S(1)} %bitcast.12, f32[64,128]{1,0:T(8,128)S(1)} %bitcast.13, f32[1,16]{1,0:T(1,128)S(1)} %bitcast.15, f32[1,16]{1,0:T(1,128)S(1)} %bitcast.16, f32[1,32]{1,0:T(1,128)S(1)} %bitcast.17, ...), custom_call_target="tpu_custom_call" | custom-call | tf_op jit(solution)/shard_map/reacting_step/pallas_call | solution.py:515
  69.7 0.8 %copy.16 = f32[16,8,8,128]{3,2,1,0:T(8,128)} copy(f32[16,8,8,128]{3,2,1,0:T(8,128)S(1)} %bitcast.11) | data formatting | bytes 1048576
  70.4 0.6 copy.17
Async XLA Ops:
  0.6 0.9 %copy-start.8 = (f32[128]{0:T(128)S(1)}, f32[128]{0:T(128)}, u32[]{:S(2)}) copy-start(f32[128]{0:T(128)} %param.17) | copy-start | bytes 1540
  0.6 0.9 %copy-start.9 = (f32[128]{0:T(128)S(1)}, f32[128]{0:T(128)}, u32[]{:S(2)}) copy-start(f32[128]{0:T(128)} %param.18) | copy-start | bytes 1540
  0.7 0.9 %copy-start.5 = (f32[16]{0:T(128)S(1)}, f32[16]{0:T(128)}, u32[]{:S(2)}) copy-start(f32[16]{0:T(128)} %param.14) | copy-start | bytes 196
  0.7 0.9 %copy-start.6 = (f32[16]{0:T(128)S(1)}, f32[16]{0:T(128)}, u32[]{:S(2)}) copy-start(f32[16]{0:T(128)} %param.15) | copy-start | bytes 196
  0.7 0.9 %copy-start.7 = (f32[32]{0:T(128)S(1)}, f32[32]{0:T(128)}, u32[]{:S(2)}) copy-start(f32[32]{0:T(128)} %param.16) | copy-start | bytes 388
  0.7 0.9 %copy-start.2 = (f32[8,8,128]{2,1,0:T(8,128)S(1)}, f32[8,8,128]{2,1,0:T(8,128)}, u32[]{:S(2)}) copy-start(f32[8,8,128]{2,1,0:T(8,128)} %param.12) | copy-start | bytes 98308
  0.7 0.9 %copy-start.3 = (f32[8,8,128]{2,1,0:T(8,128)S(1)}, f32[8,8,128]{2,1,0:T(8,128)}, u32[]{:S(2)}) copy-start(f32[8,8,128]{2,1,0:T(8,128)} %param.13) | copy-start | bytes 98308
  0.7 0.9 %copy-start.4 = (s32[32,128]{1,0:T(8,128)S(1)}, s32[32,128]{1,0:T(8,128)}, u32[]{:S(2)}) copy-start(s32[32,128]{1,0:T(8,128)} %refs_9_.1) | copy-start | bytes 49156
  1.7 1.2 %copy-start = (f32[32,8,8,128]{3,2,1,0:T(8,128)S(1)}, f32[32,8,8,128]{3,2,1,0:T(8,128)}, u32[]{:S(2)}) copy-start(f32[32,8,8,128]{3,2,1,0:T(8,128)} %param.11) | copy-start | bytes 3145732
  2.9 1.0 %copy-start.1 = (f32[576,128]{1,0:T(8,128)S(1)}, f32[576,128]{1,0:T(8,128)}, u32[]{:S(2)}) copy-start(f32[576,128]{1,0:T(8,128)} %constant.2.clone.refs_10_) | copy-start | bytes 884740

commit v2 on v1

v2 whole, which is shorter than its diff:
```python
import functools

import jax
import jax.numpy as jnp
import ml_dtypes
import numpy as np
from jax import lax
from jax.experimental import pallas as pl
from jax.experimental.pallas import tpu as pltpu
from jax.sharding import PartitionSpec as P

MESH = pl.DeviceIdType.MESH
F32 = jnp.float32
BF16 = jnp.bfloat16
NZ = 12
XY = 64
NS = 16
DIRS = ((-1, 0), (1, 0), (0, -1), (0, 1), (-1, -1), (-1, 1), (1, -1), (1, 1))
OPPOSITE = (1, 0, 3, 2, 7, 6, 5, 4)
SPOTS = (
    [p for p in range(8)],
    [56 + p for p in range(8)],
    [8 * p for p in range(8)],
    [8 * p + 7 for p in range(8)],
    [0],
    [7],
    [56],
    [63],
)

EDGES = (
    (1, 0, (1, 0), 6),
    (1, 7, (1, 0), 6),
    (0, 0, (0, 1), 8),
    (7, 0, (0, 1), 8),
)
LOG2E = 1.4426950408889634


def legendre_seven(points):
    return (429.0 * points**7 - 693.0 * points**5 + 315.0 * points**3 - 35.0 * points) / 16.0


def gll_tables():
    gll_nodes = np.array(
        [
            -1.0,
            -0.8717401485096066,
            -0.5917001814331423,
            -0.2092992179024789,
            0.2092992179024789,
            0.5917001814331423,
            0.8717401485096066,
            1.0,
        ]
    )
    at_nodes = legendre_seven(gll_nodes)
    weights = 2.0 / (56.0 * at_nodes * at_nodes)
    derivative = np.zeros((8, 8))
    for row_index in range(8):
        for col_index in range(8):
            if row_index != col_index:
                derivative[row_index, col_index] = at_nodes[row_index] / (
                    at_nodes[col_index] * (gll_nodes[row_index] - gll_nodes[col_index])
                )
    derivative[0, 0] = -14.0
    derivative[7, 7] = 14.0
    return (derivative, weights)


def constant_table():
    derivative, weights = gll_tables()
    d32 = derivative.astype(np.float32)
    w32 = weights.astype(np.float32)
    square = d32 * d32
    eye8 = np.eye(8, dtype=np.float32)
    eye16 = np.eye(16, dtype=np.float32)
    plane = np.kron(square.T, eye8) + np.kron(eye8, square.T)
    mass = (w32[:, None, None] * w32[None, :, None]) * np.tile(w32, 16)[None, None, :]
    ends = np.array([2.0, 1, 1, 1, 1, 1, 1, 2.0], np.float32)
    mult = (ends[:, None, None] * ends[None, :, None]) * np.tile(ends, 16)[None, None, :]
    mass, mult = mass.reshape(64, 128), mult.reshape(64, 128)
    return np.concatenate(
        [mass, mult, 1.0 / mult, np.pad(plane, ((0, 0), (0, 64))), np.kron(eye16, square)], 0
    ).astype(np.float32)


MASS, MULT, SHARE, PLANE, SQUARE = 0, 64, 128, 192, 256


def slope_table():
    along_z = np.kron(np.eye(16, dtype=np.float32), gll_tables()[0].astype(np.float32))
    both = []
    for matrix in (along_z.T, along_z):
        first = matrix.astype(ml_dtypes.bfloat16)
        rest = matrix - first.astype(np.float32)
        second = rest.astype(ml_dtypes.bfloat16)
        third = (rest - second.astype(np.float32)).astype(ml_dtypes.bfloat16)
        both.append(
            np.concatenate(
                [
                    np.concatenate([first, first], 0),
                    np.concatenate([second, second], 0),
                    np.concatenate([third, first], 0),
                ],
                1,
            )
        )
    return np.stack(both)


def half_matrices(matrix):
    flipped = matrix[:4, ::-1][:, :4]
    even = 0.5 * (matrix[:4, :4] + flipped)
    odd = 0.5 * (matrix[:4, :4] - flipped)
    return [[float(np.float32(v)) for v in row] for row in even], [
        [float(np.float32(v)) for v in row] for row in odd
    ]


FORWARD = half_matrices(gll_tables()[0])
BACKWARD = half_matrices(gll_tables()[0].T)


def apply_line(values, halves):
    even_mat, odd_mat = halves
    even = [values[j] + values[7 - j] for j in range(4)]
    odd = [values[j] - values[7 - j] for j in range(4)]
    low, high = [], []
    for i in range(4):
        first = even_mat[i][0] * even[0]
        second = odd_mat[i][0] * odd[0]
        for j in range(1, 4):
            first = first + even_mat[i][j] * even[j]
            second = second + odd_mat[i][j] * odd[j]
        low.append(second + first)
        high.append(second - first)
    return low + high[::-1]


def stiff_line(values, weights):
    slopes = apply_line(values, FORWARD)
    return apply_line([s * w for s, w in zip(slopes, weights)], BACKWARD)


def pieces(value):
    first = value.astype(BF16)
    rest = value - first.astype(F32)
    second = rest.astype(BF16)
    third = (rest - second.astype(F32)).astype(BF16)
    return first, second, third


def kernel(nz, ny, ng, *refs):
    ins, outs, rest = refs[:12], refs[12:14], refs[14:]
    loads, rest = rest[:12], rest[12:]
    (
        ee_ref,
        cc_ref,
        g_ref,
        wrow_ref,
        diag_ref,
        div_ref,
        my_ref,
        mp_ref,
        wb_ref,
        hm_ref,
        inv_ref,
        z_ref,
        v_ref,
        y_ref,
        sface,
        scorn,
        rface,
        rcorn,
        lface,
        lcorn,
        srow,
        rrow,
        load_sem,
        send_sem,
        recv_sem,
        row_send,
        row_recv,
    ) = rest
    share, heat, cond, diff1, helm1, expn1, loga1, ea1, kin, chg, table, slopes = loads
    out_ref, divout_ref = outs

    gx = lax.axis_index("gx")
    gy = lax.axis_index("gy")
    at_y = lax.div(gx, nz)
    at_z = lax.rem(gx, nz)
    nx = nz * ny

    def neighbour(d):
        sx, sy = DIRS[d]
        return (lax.rem(gx + (sx + nx), nx), lax.rem(gy + (sy + ng), ng))

    def peer_g(k):
        return (gx, lax.rem(gy + k, ng))

    def peer_y(k):
        return (lax.rem(at_y + k, ny) * nz + at_z, gy)

    def peer_z(k):
        return (at_y * nz + lax.rem(at_z + k, nz), gy)

    barrier = pltpu.get_barrier_semaphore()
    greeted = [neighbour(d) for d in range(8)]
    greeted += [peer_g(k) for k in range(1, ng)]
    greeted += [peer_y(k) for k in range(1, ny)]
    greeted += [peer_z(k) for k in range(1, nz)]

    fetch = [pltpu.make_async_copy(ins[i], loads[i], load_sem.at[i]) for i in range(12)]
    for one in fetch:
        one.start()
    for device in greeted:
        pl.semaphore_signal(barrier, inc=1, device_id=device, device_id_type=MESH)
    for one in fetch[1:11]:
        one.wait()

    lane = lax.broadcasted_iota(jnp.int32, (NS, 128), 1)
    sub = lax.broadcasted_iota(jnp.int32, (NS, 128), 0)

    def column(row, rows):
        at_lane = lax.broadcasted_iota(jnp.int32, (rows, row.shape[1]), 1)
        at_sub = lax.broadcasted_iota(jnp.int32, (rows, row.shape[1]), 0)
        spread = jnp.broadcast_to(row, (rows, row.shape[1]))
        return jnp.sum(jnp.where(at_lane == at_sub, spread, 0.0), axis=1, keepdims=True)

    def zsum(value):
        before = pltpu.roll(value, 1, 1)
        after = pltpu.roll(value, 127, 1)
        node = lax.broadcasted_iota(jnp.int32, value.shape, 1) & 7
        return value + jnp.where(node == 0, before, jnp.where(node == 7, after, 0.0))

    def rows(ref, first, count):
        return jnp.stack([jnp.broadcast_to(ref[pl.ds(first + i, 1), :], (NS, 128)) for i in range(count)])

    diff = jnp.broadcast_to(column(diff1[...], NS), (NS, 128))
    helm = jnp.broadcast_to(column(helm1[...], NS), (NS, 128))

    scaled = LOG2E * ea1[...]
    ea_p = [p.astype(F32) for p in pieces(-scaled)]
    co_p = [p.astype(F32) for p in pieces(LOG2E * loga1[...] + scaled)]
    sub32 = lax.broadcasted_iota(jnp.int32, (32, 128), 0)
    extra = jnp.zeros((32, 128), F32)
    for i, row in enumerate([ea_p[0], ea_p[0], ea_p[0], ea_p[1], ea_p[1], ea_p[2], *co_p]):
        extra = jnp.where(sub32 == i, row, extra)
    order = kin[...].astype(F32)
    ee_ref[...] = jnp.transpose(jnp.concatenate([order, order, order, extra], axis=0)).astype(BF16)
    change = chg[...].astype(F32)
    weighted = jnp.sum(column(expn1[...], 32) * change, axis=0, keepdims=True)
    we_p = [p.astype(F32) for p in pieces(weighted)]
    tail = jnp.where(
        sub == 0, we_p[0], jnp.where(sub == 1, we_p[1], jnp.where(sub == 2, we_p[2], 0.0))
    )
    made_by = jnp.concatenate([change[:NS], tail], axis=0).astype(BF16)
    cc_ref[:, 0:128] = made_by
    cc_ref[:, 128:256] = made_by

    inverse = 1.0 / heat[...]
    in_p = pieces(inverse)
    for i in range(3):
        g_ref[i] = in_p[i].astype(F32)
    g_ref[3] = inverse * table[MASS : MASS + 64, :]

    wrow_ref[...] = cond[...] * table[MASS : MASS + 64, :]
    diag_ref[...] = jnp.dot(
        table[PLANE : PLANE + 64, 0:64],
        wrow_ref[...],
        precision=lax.Precision.HIGHEST,
        preferred_element_type=F32,
    ) + jnp.dot(
        wrow_ref[...],
        table[SQUARE : SQUARE + 128, :],
        precision=lax.Precision.HIGHEST,
        preferred_element_type=F32,
    )
    fetch[0].wait()

    def chem(first, x, y):
        logs, gparts = [], []
        for j in range(4):
            own = share[pl.ds(first + j, 32, stride=XY), :]
            my_ref[x, y + j] = table[pl.ds(MASS + first + j, 1), :] * own[:NS]
            logs.append(LOG2E * jnp.log(own))
            part = [jnp.broadcast_to(g_ref[i, pl.ds(first + j, 1), :], (NS, 128)) for i in range(3)]
            gparts.append(
                jnp.where(
                    (sub == 0) | (sub == 3) | (sub == 5),
                    part[0],
                    jnp.where((sub == 1) | (sub == 4), part[1], jnp.where(sub == 2, part[2], 1.0)),
                )
            )
        log_p = pieces(jnp.concatenate(logs, axis=1))
        gpart = jnp.concatenate(gparts, axis=1).astype(BF16)
        stacked = jnp.concatenate([*log_p, gpart, gpart], axis=0)
        prog = jnp.exp2(jnp.dot(ee_ref[...], stacked, preferred_element_type=F32))
        high = prog.astype(BF16)
        low = (prog - high.astype(F32)).astype(BF16)
        made = jnp.dot(
            cc_ref[...], jnp.concatenate([high, low], axis=0), preferred_element_type=F32
        )
        for j in range(4):
            at = first + j
            here = made[:, 128 * j : 128 * (j + 1)]
            mp_ref[x, y + j] = table[pl.ds(MASS + at, 1), :] * here[:NS]
            total = here[16:17] + here[17:18] + here[18:19]
            div_ref[pl.ds(at, 1), :] = total * g_ref[3, pl.ds(at, 1), :]

    def chem_plane(x):
        chem(8 * x, x, 0)
        chem(8 * x + 4, x, 4)

    def chem_ends(i, carry):
        chem_plane(7 * i)
        return carry

    def chem_mid(i, carry):
        chem_plane(1 + i)
        return carry

    def pack(stage, d, field, scalar):
        spots = SPOTS[d]
        if d < 4:
            for p, at in enumerate(spots):
                sface[stage, d, 16 * p : 16 * p + 16, :] = field(at)
            sface[stage, d, 128:136, :] = scalar[pl.ds(spots[0], 8, stride=spots[1] - spots[0]), :]
        else:
            at = spots[0]
            scorn[stage, d - 4, 0:16, :] = field(at)
            scorn[stage, d - 4, 16:24, :] = jnp.broadcast_to(scalar[at : at + 1, :], (8, 128))

    started = []

    def launch(stage, d, source, target):
        copy = pltpu.make_async_remote_copy(
            src_ref=source,
            dst_ref=target,
            send_sem=send_sem.at[8 * stage + d],
            recv_sem=recv_sem.at[8 * stage + d],
            device_id=neighbour(d),
            device_id_type=MESH,
        )
        copy.start()
        started.append((stage, d, copy))

    def send(stage, d, field, scalar):
        pack(stage, d, field, scalar)
        if d < 4:
            launch(stage, d, sface.at[stage, d], rface.at[stage, d])
        else:
            launch(stage, d, scorn.at[stage, d - 4], rcorn.at[stage, d - 4])

    def await_from(stage, which):
        for at_stage, d, copy in started:
            if at_stage == stage and d in which:
                copy.wait_recv()

    def add_scalars(stage, scalar):
        for d in range(8):
            spots = SPOTS[OPPOSITE[d]]
            if d < 4:
                where = pl.ds(spots[0], 8, stride=spots[1] - spots[0])
                scalar[where, :] = scalar[where, :] + rface[stage, d, 128:136, :]
            else:
                at = spots[0]
                scalar[at : at + 1, :] = scalar[at : at + 1, :] + rcorn[stage, d - 4, 16:17, :]

    def arrived(stage, x, y):
        parts = []
        for d in range(8):
            spots = SPOTS[OPPOSITE[d]]
            if 8 * x + y not in spots:
                continue
            p = spots.index(8 * x + y)
            if stage == 2:
                parts.append(lface[d, p] if d < 4 else lcorn[d - 4])
            elif d < 4:
                parts.append(rface[stage, d, 16 * p : 16 * p + 16, :])
            else:
                parts.append(rcorn[stage, d - 4, 0:16, :])
        return functools.reduce(lambda a, b: a + b, parts)

    def my_spot(at):
        return table[MASS + at : MASS + at + 1, :] * share[pl.ds(at, NS, stride=XY), :]

    def mp_spot(at):
        return mp_ref[at // 8, at % 8]

    lax.fori_loop(0, 2, chem_ends, 0)
    pl.semaphore_wait(barrier, len(greeted))
    for d in range(8):
        send(0, d, my_spot, diag_ref)
    for d in (0, 1, 4, 5, 6, 7):
        send(1, d, mp_spot, div_ref)
    lax.fori_loop(0, 6, chem_mid, 0)
    for d in (2, 3):
        send(1, d, mp_spot, div_ref)

    none = jnp.zeros((NS, 128), F32)

    await_from(0, range(8))
    add_scalars(0, diag_ref)
    for x in range(8):
        diag_ref[8 * x : 8 * x + 8, :] = zsum(diag_ref[8 * x : 8 * x + 8, :])

    def invert(x, carry):
        wb_ref[x] = rows(wrow_ref, 8 * x, 8)
        hm = helm * rows(table, MASS + 8 * x, 8)
        hm_ref[x] = hm
        inv_ref[x] = 1.0 / (diff * rows(diag_ref, 8 * x, 8) + hm * rows(table, MULT + 8 * x, 8))
        return carry

    lax.fori_loop(0, 8, invert, 0)

    def divergence(x):
        here = slice(8 * x, 8 * x + 8)
        norm = table[MASS + 8 * x : MASS + 8 * x + 8, :] * table[MULT + 8 * x : MULT + 8 * x + 8, :]
        divout_ref[here, :] = zsum(div_ref[here, :]) / norm

    def flat_zsum(value):
        return zsum(value.reshape(-1, 128)).reshape(value.shape)

    def begin(x, y, step, count, made, carried, acc):
        first, jump = 8 * x + y, 8 * step[0] + step[1]
        spots = [(x + i * step[0], y + i * step[1]) for i in range(count)]
        div = jnp.stack(
            [jnp.broadcast_to(divout_ref[pl.ds(first + i * jump, 1), :], (NS, 128)) for i in range(count)]
        )
        part = jnp.stack(
            [
                jnp.broadcast_to(table[pl.ds(SHARE + first + i * jump, 1), :], (NS, 128))
                for i in range(count)
            ]
        )
        resid = flat_zsum(made + (helm - div) * carried)
        inv = jnp.stack([inv_ref[a, b] for a, b in spots])
        precond = inv * resid
        for i, (a, b) in enumerate(spots):
            z_ref[a, b] = precond[i]
        return acc + jnp.sum(resid * precond * part, axis=0)

    def advance(x, y, step, count, image, acc):
        first, jump = 8 * x + y, 8 * step[0] + step[1]
        spots = [(x + i * step[0], y + i * step[1]) for i in range(count)]
        part = jnp.stack(
            [
                jnp.broadcast_to(table[pl.ds(SHARE + first + i * jump, 1), :], (NS, 128))
                for i in range(count)
            ]
        )
        image = flat_zsum(image)
        inv = jnp.stack([inv_ref[a, b] for a, b in spots])
        precond = inv * image
        for i, (a, b) in enumerate(spots):
            v_ref[a, b] = precond[i]
        return acc + jnp.sum(image * precond * part, axis=0)

    def with_edges(field, stage, x, y, step, count):
        spots = [(x + i * step[0], y + i * step[1]) for i in range(count)]
        return jnp.stack([field[a, b] + arrived(stage, a, b) for a, b in spots])

    for x in range(1, 7):
        divergence(x)

    def begin_inside(i, acc):
        x = 1 + i
        return begin(x, 1, (0, 1), 6, mp_ref[x, 1:7], my_ref[x, 1:7], acc)

    dot_a = lax.fori_loop(0, 6, begin_inside, none)
    await_from(1, range(8))
    add_scalars(1, div_ref)
    for x in range(8):
        divergence(x)
    for x, y, step, count in EDGES:
        made = with_edges(mp_ref, 1, x, y, step, count)
        carried = with_edges(my_ref, 0, x, y, step, count)
        dot_a = begin(x, y, step, count, made, carried, dot_a)

    fetch[11].wait()

    def slope_product(value, which):
        first, second, third = pieces(value)
        wide = jnp.dot(
            jnp.concatenate([first, second], axis=1),
            slopes[which, :, 0:256],
            preferred_element_type=F32,
        )
        thin = jnp.dot(
            jnp.concatenate([first, third], axis=1),
            slopes[which, :, 256:384],
            preferred_element_type=F32,
        )
        return wide[:, 0:128] + wide[:, 128:256] + thin

    def yz_part(planes, weights):
        value = jnp.concatenate([p.reshape(128, 128) for p in planes], axis=0)
        weight = jnp.concatenate([w.reshape(128, 128) for w in weights], axis=0)
        back = slope_product(slope_product(value, 0) * weight, 1)
        result = []
        for i, (p, w) in enumerate(zip(planes, weights)):
            lines = jnp.stack(stiff_line([p[y] for y in range(8)], [w[y] for y in range(8)]))
            result.append(back[128 * i : 128 * (i + 1)].reshape(8, NS, 128) + lines)
        return result

    def operate(source, faces_done):
        planes = [source[0], source[7]]
        got = yz_part(planes, [wb_ref[0], wb_ref[7]])
        y_ref[0] = got[0]
        y_ref[7] = got[1]

        def x_part(y, acc):
            values = [source[x, y] for x in range(8)]
            got = stiff_line(values, [wb_ref[x, y] for x in range(8)])
            for x in range(1, 7):
                y_ref[x, y] = got[x]
            for x in (0, 7):
                image = diff * (y_ref[x, y] + got[x]) + hm_ref[x, y] * values[x]
                y_ref[x, y] = image
                acc = acc + values[x] * image
            return acc

        total = lax.fori_loop(0, 8, x_part, none)
        faces_done()

        def rest_part(i, acc):
            first = 1 + 2 * i
            planes = [source[first], source[first + 1]]
            got = yz_part(planes, [wb_ref[first], wb_ref[first + 1]])
            for j in range(2):
                image = diff * (y_ref[first + j] + got[j]) + hm_ref[first + j] * planes[j]
                y_ref[first + j] = image
                acc = acc + jnp.sum(planes[j] * image, axis=0)
            return acc

        return lax.fori_loop(0, 3, rest_part, total)

    def send_faces():
        for d, x in ((0, 0), (1, 7)):
            launch(2, d, y_ref.at[x], lface.at[d])
        for d in range(4, 8):
            at = SPOTS[d][0]
            launch(2, d, y_ref.at[at // 8, at % 8], lcorn.at[d - 4])

    dot_c = operate(z_ref, send_faces)
    for d, y in ((2, 0), (3, 7)):
        launch(2, d, y_ref.at[:, y], lface.at[d])

    def advance_inside(i, acc):
        x = 1 + i
        return advance(x, 1, (0, 1), 6, y_ref[x, 1:7], acc)

    dot_b = lax.fori_loop(0, 6, advance_inside, none)
    await_from(2, range(8))
    for x, y, step, count in EDGES:
        dot_b = advance(x, y, step, count, with_edges(y_ref, 2, x, y, step, count), dot_b)
    for stage, _, copy in started:
        copy.wait_send()
    dot_d = operate(v_ref, lambda: None)

    packed = none
    for q, acc in enumerate((dot_a, dot_c, dot_b, dot_d)):
        packed = packed + jnp.where(lane == 16 * q + sub, jnp.sum(acc, axis=1, keepdims=True), 0.0)
    row = jnp.sum(packed, axis=0, keepdims=True)

    rows_sent = []
    slot = 0
    for phase, (count, peer) in enumerate(((ng, peer_g), (ny, peer_y), (nz, peer_z))):
        srow[phase] = row
        copies = []
        for k in range(1, count):
            copy = pltpu.make_async_remote_copy(
                src_ref=srow.at[phase],
                dst_ref=rrow.at[slot],
                send_sem=row_send.at[slot],
                recv_sem=row_recv.at[slot],
                device_id=peer(k),
                device_id_type=MESH,
            )
            copy.start()
            copies.append((slot, copy))
            slot += 1
        for _, copy in copies:
            copy.wait_recv()
        for at, _ in copies:
            row = row + rrow[at]
        rows_sent += [copy for _, copy in copies]

    totals = jnp.broadcast_to(row, (NS, 128))
    a, c, b, d = [
        jnp.sum(jnp.where(lane == 16 * q + sub, totals, 0.0), axis=1, keepdims=True) for q in range(4)
    ]
    ratio = b / c
    gamma = (c - ratio * a) / (d - ratio * b)
    alpha = a / c - gamma * ratio
    alpha = jnp.broadcast_to(alpha, (NS, 128))
    gamma = jnp.broadcast_to(gamma, (NS, 128))

    def finish(x, carry):
        for y in range(8):
            out_ref[pl.ds(8 * x + y, NS, stride=XY), :] = alpha * z_ref[x, y] + gamma * v_ref[x, y]
        return carry

    lax.fori_loop(0, 8, finish, 0)
    for copy in rows_sent:
        copy.wait_send()


def shards(nz, ny, ng, *args):
    share, heat, cond, diff, helm, expn, loga, ea, kin, chg = args
    count = (ng - 1) + (ny - 1) + (nz - 1)
    operands = [
        share.reshape(32 * XY, 128),
        heat.reshape(XY, 128),
        cond.reshape(XY, 128),
        diff.reshape(1, NS),
        helm.reshape(1, NS),
        expn.reshape(1, 32),
        loga.reshape(1, 128),
        ea.reshape(1, 128),
        kin.T,
        chg,
        jnp.asarray(constant_table()),
        jnp.asarray(slope_table()),
    ]
    cube = pltpu.VMEM((8, 8, NS, 128), F32)
    out, div = pl.pallas_call(
        functools.partial(kernel, nz, ny, ng),
        out_shape=(
            jax.ShapeDtypeStruct((NS * XY, 128), F32),
            jax.ShapeDtypeStruct((XY, 128), F32),
        ),
        in_specs=[pl.BlockSpec(memory_space=pltpu.HBM)] * 12,
        out_specs=(
            pl.BlockSpec(memory_space=pltpu.VMEM),
            pl.BlockSpec(memory_space=pltpu.VMEM),
        ),
        scratch_shapes=[pltpu.VMEM(o.shape, o.dtype) for o in operands]
        + [
            pltpu.VMEM((128, 128), BF16),
            pltpu.VMEM((32, 256), BF16),
            pltpu.VMEM((4, XY, 128), F32),
            pltpu.VMEM((XY, 128), F32),
            pltpu.VMEM((XY, 128), F32),
            pltpu.VMEM((XY, 128), F32),
        ]
        + [cube] * 8
        + [
            pltpu.VMEM((2, 4, 136, 128), F32),
            pltpu.VMEM((2, 4, 24, 128), F32),
            pltpu.VMEM((2, 4, 136, 128), F32),
            pltpu.VMEM((2, 4, 24, 128), F32),
            pltpu.VMEM((4, 8, NS, 128), F32),
            pltpu.VMEM((4, NS, 128), F32),
            pltpu.VMEM((3, 1, 128), F32),
            pltpu.VMEM((count, 1, 128), F32),
            pltpu.SemaphoreType.DMA((12,)),
            pltpu.SemaphoreType.DMA((24,)),
            pltpu.SemaphoreType.DMA((24,)),
            pltpu.SemaphoreType.DMA((count,)),
            pltpu.SemaphoreType.DMA((count,)),
        ],
        compiler_params=pltpu.CompilerParams(
            collective_id=0, has_side_effects=True, vmem_limit_bytes=40 * 1024 * 1024
        ),
        name="reacting_step",
    )(*operands)
    return out.reshape(NS, 8, 8, 128), div.reshape(8, 8, 128)


def solution(mesh):
    ng = mesh.shape["gy"]
    ny = mesh.shape["gx"] // NZ
    field = P("gx", "gy", None)
    species = P(None, "gx", "gy", None)
    return jax.shard_map(
        functools.partial(shards, NZ, ny, ng),
        mesh=mesh,
        in_specs=(species, field, field, P(), P(), P(), P(), P(), P(), P()),
        out_specs=(species, field),
        check_vma=False,
    )
```

time: 71.8 us -> 59.9 us (0.83)
  Pallas kernels: 65.8 us -> 49 us
  local copies, waits for them, and re-layouts: 4.48 us -> 9.45 us
    pallas_call x1, Pallas kernels: 65.8 us -> 49 us  [shards(): pl.pallas_call(functools.partial(kernel, nz, ny, ng), out_shape=(jax.Shap...]
    unnamed x23 -> x26, local copies, waits for them, and re-layouts: 4.48 us -> 9.45 us
where the time goes in v2:
time: 59.9 us; the launch traced here: 59.2 us
  Pallas kernels  49 us (82%)
  local copies, waits for them, and re-layouts  9.45 us (16%)
  between operations  0.68 us (1%)
    pallas_call x1, Pallas kernels, shards(): pl.pallas_call(functools.partial(kernel, nz, ny, ng), out_shape=(jax.Shap...  49 us
    unnamed x26, local copies, waits for them, and re-layouts  9.45 us

profile of v2, /device:TPU:1, one launch (start us, length us, event | category | flops | bytes accessed | tf_op | source)
XLA Modules:
  0.0 59.2 jit_solution(4235294592219170918)
XLA Ops:
  0.6 0.0 copy-start.5
  0.6 0.0 copy-start.7
  0.7 0.0 copy-start.8
  0.7 0.7 %copy-done.5 = s32[128,32]{0,1:T(8,128)S(1)} copy-done((s32[128,32]{0,1:T(8,128)S(1)}, s32[128,32]{0,1:T(8,128)}, u32[]{:S(2)}) %copy-start.5) | copy-done | bytes 16408
  1.4 0.0 copy-done.7
  1.4 0.0 copy-done.8
  1.4 0.0 copy-start
  1.4 1.2 %copy-done = f32[32,8,8,128]{3,2,1,0:T(8,128)S(1)} copy-done((f32[32,8,8,128]{3,2,1,0:T(8,128)S(1)}, f32[32,8,8,128]{3,2,1,0:T(8,128)}, u32[]{:S(2)}) %copy-start) | copy-done | bytes 1048600
  2.6 0.0 copy-start.1
  2.6 1.0 %copy-done.1 = bf16[2,256,384]{2,1,0:T(8,128)(2,1)S(1)} copy-done((bf16[2,256,384]{2,1,0:T(8,128)(2,1)S(1)}, bf16[2,256,384]{2,1,0:T(8,128)(2,1)}, u32[]{:S(2)}) %copy-start.1) | copy-done | bytes 393240
  3.6 0.0 copy-start.2
  3.6 0.9 %copy-done.2 = f32[384,128]{1,0:T(8,128)S(1)} copy-done((f32[384,128]{1,0:T(8,128)S(1)}, f32[384,128]{1,0:T(8,128)}, u32[]{:S(2)}) %copy-start.2) | copy-done | bytes 196632
  4.5 0.0 copy-start.3
  4.5 0.8 %copy-done.3 = f32[8,8,128]{2,1,0:T(8,128)S(1)} copy-done((f32[8,8,128]{2,1,0:T(8,128)S(1)}, f32[8,8,128]{2,1,0:T(8,128)}, u32[]{:S(2)}) %copy-start.3) | copy-done | bytes 32792
  5.3 0.0 copy-start.4
  5.3 0.8 %copy-done.4 = f32[8,8,128]{2,1,0:T(8,128)S(1)} copy-done((f32[8,8,128]{2,1,0:T(8,128)S(1)}, f32[8,8,128]{2,1,0:T(8,128)}, u32[]{:S(2)}) %copy-start.4) | copy-done | bytes 32792
  6.0 0.0 copy-start.6
  6.0 0.7 %copy-done.6 = s32[32,128]{1,0:T(8,128)S(1)} copy-done((s32[32,128]{1,0:T(8,128)S(1)}, s32[32,128]{1,0:T(8,128)}, u32[]{:S(2)}) %copy-start.6) | copy-done | bytes 16408
  6.7 0.7 %copy-done.9 = f32[32]{0:T(128)S(1)} copy-done((f32[32]{0:T(128)S(1)}, f32[32]{0:T(128)}, u32[]{:S(2)}) %copy-start.9) | copy-done | bytes 152
  7.4 0.7 %copy-done.10 = f32[128]{0:T(128)S(1)} copy-done((f32[128]{0:T(128)S(1)}, f32[128]{0:T(128)}, u32[]{:S(2)}) %copy-start.10) | copy-done | bytes 536
  8.1 0.7 %copy-done.11 = f32[128]{0:T(128)S(1)} copy-done((f32[128]{0:T(128)S(1)}, f32[128]{0:T(128)}, u32[]{:S(2)}) %copy-start.11) | copy-done | bytes 536
  8.7 49.0 %reacting_step.1 = (f32[1024,128]{1,0:T(8,128)S(1)}, f32[64,128]{1,0:T(8,128)S(1)}) custom-call(f32[2048,128]{1,0:T(8,128)S(1)} %bitcast.11, f32[64,128]{1,0:T(8,128)S(1)} %bitcast.13, f32[64,128]{1,0:T(8,128)S(1)} %bitcast.14, f32[1,16]{1,0:T(1,128)S(1)} %bitcast.17, f32[1,16]{1,0:T(1,128)S(1)} %bitcast.18, f32[1,32]{1,0:T(1,128)S(1)} %bitcast.19, ...), custom_call_target="tpu_custom_call" | custom-call | tf_op jit(solution)/shard_map/reacting_step/pallas_call | solution.py:629
  57.8 0.8 %copy.16 = f32[16,8,8,128]{3,2,1,0:T(8,128)} copy(f32[16,8,8,128]{3,2,1,0:T(8,128)S(1)} %bitcast.12) | data formatting | bytes 1048576
  58.6 0.6 %copy.17 = f32[8,8,128]{2,1,0:T(8,128)} copy(f32[8,8,128]{2,1,0:T(8,128)S(1)} %bitcast.15) | data formatting | bytes 65536
  (3 shorter events, 0.0 us)
Async XLA Ops:
  0.6 0.7 %copy-start.5 = (s32[128,32]{0,1:T(8,128)S(1)}, s32[128,32]{0,1:T(8,128)}, u32[]{:S(2)}) copy-start(s32[128,32]{0,1:T(8,128)} %param.20) | copy-start | bytes 49156
  0.6 0.7 %copy-start.7 = (f32[16]{0:T(128)S(1)}, f32[16]{0:T(128)}, u32[]{:S(2)}) copy-start(f32[16]{0:T(128)} %param.15) | copy-start | bytes 196
  0.7 0.7 %copy-start.8 = (f32[16]{0:T(128)S(1)}, f32[16]{0:T(128)}, u32[]{:S(2)}) copy-start(f32[16]{0:T(128)} %param.16) | copy-start | bytes 196
  1.4 1.2 %copy-start = (f32[32,8,8,128]{3,2,1,0:T(8,128)S(1)}, f32[32,8,8,128]{3,2,1,0:T(8,128)}, u32[]{:S(2)}) copy-start(f32[32,8,8,128]{3,2,1,0:T(8,128)} %param.12) | copy-start | bytes 3145732
  2.6 1.0 %copy-start.1 = (bf16[2,256,384]{2,1,0:T(8,128)(2,1)S(1)}, bf16[2,256,384]{2,1,0:T(8,128)(2,1)}, u32[]{:S(2)}) copy-start(bf16[2,256,384]{2,1,0:T(8,128)(2,1)} %constant.5.clone.refs_11_) | copy-start | bytes 1179652
  3.6 0.9 %copy-start.2 = (f32[384,128]{1,0:T(8,128)S(1)}, f32[384,128]{1,0:T(8,128)}, u32[]{:S(2)}) copy-start(f32[384,128]{1,0:T(8,128)} %constant.4.clone.refs_10_) | copy-start | bytes 589828
  4.5 0.8 %copy-start.3 = (f32[8,8,128]{2,1,0:T(8,128)S(1)}, f32[8,8,128]{2,1,0:T(8,128)}, u32[]{:S(2)}) copy-start(f32[8,8,128]{2,1,0:T(8,128)} %param.13) | copy-start | bytes 98308
  5.3 0.8 %copy-start.4 = (f32[8,8,128]{2,1,0:T(8,128)S(1)}, f32[8,8,128]{2,1,0:T(8,128)}, u32[]{:S(2)}) copy-start(f32[8,8,128]{2,1,0:T(8,128)} %param.14) | copy-start | bytes 98308
  6.0 0.7 %copy-start.6 = (s32[32,128]{1,0:T(8,128)S(1)}, s32[32,128]{1,0:T(8,128)}, u32[]{:S(2)}) copy-start(s32[32,128]{1,0:T(8,128)} %refs_9_.1) | copy-start | bytes 49156
  6.7 0.7 %copy-start.9 = (f32[32]{0:T(128)S(1)}, f32[32]{0:T(128)}, u32[]{:S(2)}) copy-start(f32[32]{0:T(128)} %param.17) | copy-start | bytes 388
  7.4 0.7 %copy-start.10 = (f32[128]{0:T(128)S(1)}, f32[128]{0:T(128)}, u32[]{:S(2)}) copy-start(f32[128]{0:T(128)} %param.18) | copy-start | bytes 1540
  8.1 0.7 %copy-start.11 = (f32[128]{0:T(128)S(1)}, f32[128]{0:T(128)}, u32[]{:S(2)}) copy-start(f32[128]{0:T(128)} %param.19) | copy-start | bytes 1540

commit v3 on v2

--- a/solution.py
+++ b/solution.py
@@ -152,7 +152,7 @@
 
 
 def kernel(nz, ny, ng, *refs):
-    ins, outs, rest = refs[:12], refs[12:14], refs[14:]
+    ins, outs, rest = refs[:12], refs[12:17], refs[17:]
     loads, rest = rest[:12], rest[12:]
     (
         ee_ref,
@@ -169,22 +169,24 @@
         z_ref,
         v_ref,
         y_ref,
-        sface,
-        scorn,
         rface,
         rcorn,
-        lface,
-        lcorn,
+        spair,
+        rpair,
+        divout_ref,
+        zt_ref,
+        vt_ref,
         srow,
         rrow,
         load_sem,
+        store_sem,
         send_sem,
         recv_sem,
         row_send,
         row_recv,
     ) = rest
     share, heat, cond, diff1, helm1, expn1, loga1, ea1, kin, chg, table, slopes = loads
-    out_ref, divout_ref = outs
+    zt_out, vt_out, div_out, alpha_ref, gamma_ref = outs
 
     gx = lax.axis_index("gx")
     gy = lax.axis_index("gy")
@@ -279,13 +281,73 @@
     )
     fetch[0].wait()
 
-    def chem(first, x, y):
+    started = []
+
+    def launch(stage, d, source, target):
+        copy = pltpu.make_async_remote_copy(
+            src_ref=source,
+            dst_ref=target,
+            send_sem=send_sem.at[8 * stage + d],
+            recv_sem=recv_sem.at[8 * stage + d],
+            device_id=neighbour(d),
+            device_id_type=MESH,
+        )
+        copy.start()
+        started.append((stage, d, copy))
+
+    def send(stage, d, field):
+        x, y = SPOTS[d][0] // 8, SPOTS[d][0] % 8
+        if d < 2:
+            launch(stage, d, field.at[x], rface.at[stage, d])
+        elif d < 4:
+            launch(stage, d, field.at[:, y], rface.at[stage, d])
+        else:
+            launch(stage, d, field.at[x, y], rcorn.at[stage, d - 4])
+
+    def send_scalars(d):
+        spots = SPOTS[d]
+        for i, scalar in enumerate((diag_ref, div_ref)):
+            if d < 4:
+                tile = scalar[pl.ds(spots[0], 8, stride=spots[1] - spots[0]), :]
+            else:
+                tile = jnp.broadcast_to(scalar[spots[0] : spots[0] + 1, :], (8, 128))
+            spair[d, 8 * i : 8 * i + 8, :] = tile
+        launch(3, d, spair.at[d], rpair.at[d])
+
+    def await_from(stage, which):
+        for at_stage, d, copy in started:
+            if at_stage == stage and d in which:
+                copy.wait_recv()
+
+    def add_scalars():
+        for i, scalar in enumerate((diag_ref, div_ref)):
+            for d in range(8):
+                spots = SPOTS[OPPOSITE[d]]
+                if d < 4:
+                    where = pl.ds(spots[0], 8, stride=spots[1] - spots[0])
+                    scalar[where, :] = scalar[where, :] + rpair[d, 8 * i : 8 * i + 8, :]
+                else:
+                    at = spots[0]
+                    scalar[at : at + 1, :] = scalar[at : at + 1, :] + rpair[d, 8 * i : 8 * i + 1, :]
+
+    def arrived(stage, x, y):
+        parts = []
+        for d in range(8):
+            spots = SPOTS[OPPOSITE[d]]
+            if 8 * x + y in spots:
+                p = spots.index(8 * x + y)
+                parts.append(rface[stage, d, p] if d < 4 else rcorn[stage, d - 4])
+        return functools.reduce(lambda a, b: a + b, parts)
+
+    def chem(spots, inside):
         logs, gparts = [], []
-        for j in range(4):
-            own = share[pl.ds(first + j, 32, stride=XY), :]
-            my_ref[x, y + j] = table[pl.ds(MASS + first + j, 1), :] * own[:NS]
+        for x, y in spots:
+            at = 8 * x + y
+            own = share[pl.ds(at, 32, stride=XY), :]
+            if inside:
+                my_ref[x, y] = table[pl.ds(MASS + at, 1), :] * own[:NS]
             logs.append(LOG2E * jnp.log(own))
-            part = [jnp.broadcast_to(g_ref[i, pl.ds(first + j, 1), :], (NS, 128)) for i in range(3)]
+            part = [jnp.broadcast_to(g_ref[i, pl.ds(at, 1), :], (NS, 128)) for i in range(3)]
             gparts.append(
                 jnp.where(
                     (sub == 0) | (sub == 3) | (sub == 5),
@@ -302,107 +364,45 @@
         made = jnp.dot(
             cc_ref[...], jnp.concatenate([high, low], axis=0), preferred_element_type=F32
         )
-        for j in range(4):
-            at = first + j
+        for j, (x, y) in enumerate(spots):
+            at = 8 * x + y
             here = made[:, 128 * j : 128 * (j + 1)]
-            mp_ref[x, y + j] = table[pl.ds(MASS + at, 1), :] * here[:NS]
+            mp_ref[x, y] = table[pl.ds(MASS + at, 1), :] * here[:NS]
             total = here[16:17] + here[17:18] + here[18:19]
             div_ref[pl.ds(at, 1), :] = total * g_ref[3, pl.ds(at, 1), :]
 
-    def chem_plane(x):
-        chem(8 * x, x, 0)
-        chem(8 * x + 4, x, 4)
-
-    def chem_ends(i, carry):
-        chem_plane(7 * i)
+    def chem_sides(i, carry):
+        for j in range(2):
+            x = 4 * i + 2 * j
+            chem([(x, 0), (x, 7), (x + 1, 0), (x + 1, 7)], False)
         return carry
 
-    def chem_mid(i, carry):
-        chem_plane(1 + i)
+    def chem_inside(i, carry):
+        for j in range(2):
+            chem([(1 + 2 * i + j, y) for y in range(1, 7)], True)
         return carry
 
-    def pack(stage, d, field, scalar):
-        spots = SPOTS[d]
-        if d < 4:
-            for p, at in enumerate(spots):
-                sface[stage, d, 16 * p : 16 * p + 16, :] = field(at)
-            sface[stage, d, 128:136, :] = scalar[pl.ds(spots[0], 8, stride=spots[1] - spots[0]), :]
-        else:
-            at = spots[0]
-            scorn[stage, d - 4, 0:16, :] = field(at)
-            scorn[stage, d - 4, 16:24, :] = jnp.broadcast_to(scalar[at : at + 1, :], (8, 128))
-
-    started = []
-
-    def launch(stage, d, source, target):
-        copy = pltpu.make_async_remote_copy(
-            src_ref=source,
-            dst_ref=target,
-            send_sem=send_sem.at[8 * stage + d],
-            recv_sem=recv_sem.at[8 * stage + d],
-            device_id=neighbour(d),
-            device_id_type=MESH,
-        )
-        copy.start()
-        started.append((stage, d, copy))
-
-    def send(stage, d, field, scalar):
-        pack(stage, d, field, scalar)
-        if d < 4:
-            launch(stage, d, sface.at[stage, d], rface.at[stage, d])
-        else:
-            launch(stage, d, scorn.at[stage, d - 4], rcorn.at[stage, d - 4])
-
-    def await_from(stage, which):
-        for at_stage, d, copy in started:
-            if at_stage == stage and d in which:
-                copy.wait_recv()
-
-    def add_scalars(stage, scalar):
-        for d in range(8):
-            spots = SPOTS[OPPOSITE[d]]
-            if d < 4:
-                where = pl.ds(spots[0], 8, stride=spots[1] - spots[0])
-                scalar[where, :] = scalar[where, :] + rface[stage, d, 128:136, :]
-            else:
-                at = spots[0]
-                scalar[at : at + 1, :] = scalar[at : at + 1, :] + rcorn[stage, d - 4, 16:17, :]
-
-    def arrived(stage, x, y):
-        parts = []
-        for d in range(8):
-            spots = SPOTS[OPPOSITE[d]]
-            if 8 * x + y not in spots:
-                continue
-            p = spots.index(8 * x + y)
-            if stage == 2:
-                parts.append(lface[d, p] if d < 4 else lcorn[d - 4])
-            elif d < 4:
-                parts.append(rface[stage, d, 16 * p : 16 * p + 16, :])
-            else:
-                parts.append(rcorn[stage, d - 4, 0:16, :])
-        return functools.reduce(lambda a, b: a + b, parts)
-
-    def my_spot(at):
-        return table[MASS + at : MASS + at + 1, :] * share[pl.ds(at, NS, stride=XY), :]
-
-    def mp_spot(at):
-        return mp_ref[at // 8, at % 8]
-
-    lax.fori_loop(0, 2, chem_ends, 0)
+    for x in range(8):
+        for y in range(8):
+            if x in (0, 7) or y in (0, 7):
+                at = 8 * x + y
+                my_ref[x, y] = table[MASS + at : MASS + at + 1, :] * share[pl.ds(at, NS, stride=XY), :]
     pl.semaphore_wait(barrier, len(greeted))
     for d in range(8):
-        send(0, d, my_spot, diag_ref)
-    for d in (0, 1, 4, 5, 6, 7):
-        send(1, d, mp_spot, div_ref)
-    lax.fori_loop(0, 6, chem_mid, 0)
-    for d in (2, 3):
-        send(1, d, mp_spot, div_ref)
+        send(0, d, my_ref)
+    chem([(0, y) for y in range(1, 7)], False)
+    chem([(7, y) for y in range(1, 7)], False)
+    lax.fori_loop(0, 2, chem_sides, 0)
+    for d in range(8):
+        send_scalars(d)
+    for d in range(8):
+        send(1, d, mp_ref)
+    lax.fori_loop(0, 3, chem_inside, 0)
 
     none = jnp.zeros((NS, 128), F32)
 
-    await_from(0, range(8))
-    add_scalars(0, diag_ref)
+    await_from(3, range(8))
+    add_scalars()
     for x in range(8):
         diag_ref[8 * x : 8 * x + 8, :] = zsum(diag_ref[8 * x : 8 * x + 8, :])
 
@@ -462,18 +462,18 @@
         spots = [(x + i * step[0], y + i * step[1]) for i in range(count)]
         return jnp.stack([field[a, b] + arrived(stage, a, b) for a, b in spots])
 
-    for x in range(1, 7):
+    for x in range(8):
         divergence(x)
+    store_div = pltpu.make_async_copy(divout_ref, div_out, store_sem.at[0])
+    store_div.start()
 
     def begin_inside(i, acc):
         x = 1 + i
         return begin(x, 1, (0, 1), 6, mp_ref[x, 1:7], my_ref[x, 1:7], acc)
 
     dot_a = lax.fori_loop(0, 6, begin_inside, none)
+    await_from(0, range(8))
     await_from(1, range(8))
-    add_scalars(1, div_ref)
-    for x in range(8):
-        divergence(x)
     for x, y, step, count in EDGES:
         made = with_edges(mp_ref, 1, x, y, step, count)
         carried = with_edges(my_ref, 0, x, y, step, count)
@@ -538,15 +538,12 @@
         return lax.fori_loop(0, 3, rest_part, total)
 
     def send_faces():
-        for d, x in ((0, 0), (1, 7)):
-            launch(2, d, y_ref.at[x], lface.at[d])
-        for d in range(4, 8):
-            at = SPOTS[d][0]
-            launch(2, d, y_ref.at[at // 8, at % 8], lcorn.at[d - 4])
+        for d in (0, 1, 4, 5, 6, 7):
+            send(2, d, y_ref)
 
     dot_c = operate(z_ref, send_faces)
-    for d, y in ((2, 0), (3, 7)):
-        launch(2, d, y_ref.at[:, y], lface.at[d])
+    for d in (2, 3):
+        send(2, d, y_ref)
 
     def advance_inside(i, acc):
         x = 1 + i
@@ -556,15 +553,42 @@
     await_from(2, range(8))
     for x, y, step, count in EDGES:
         dot_b = advance(x, y, step, count, with_edges(y_ref, 2, x, y, step, count), dot_b)
-    for stage, _, copy in started:
-        copy.wait_send()
-    dot_d = operate(v_ref, lambda: None)
+
+    def square_x(y, acc):
+        slopes_x = apply_line([v_ref[x, y] for x in range(8)], FORWARD)
+        return acc + sum(wb_ref[x, y] * slopes_x[x] * slopes_x[x] for x in range(8))
+
+    def square_yz(i, accs):
+        acc, mass = accs
+        first = 2 * i
+        value = v_ref[pl.ds(first, 2)].reshape(256, 128)
+        slope_z = slope_product(value, 0)
+        for j in range(2):
+            plane, weight = v_ref[first + j], wb_ref[first + j]
+            slope_y = jnp.stack(apply_line([plane[y] for y in range(8)], FORWARD))
+            here = slope_z[128 * j : 128 * (j + 1)].reshape(8, NS, 128)
+            acc = acc + jnp.sum(weight * (slope_y * slope_y + here * here), axis=0)
+            mass = mass + jnp.sum(hm_ref[first + j] * plane * plane, axis=0)
+        return acc, mass
+
+    stiff, mass = lax.fori_loop(0, 4, square_yz, (none, none))
+    stiff = lax.fori_loop(0, 8, square_x, stiff)
+    dot_d = diff * stiff + mass
 
     packed = none
     for q, acc in enumerate((dot_a, dot_c, dot_b, dot_d)):
         packed = packed + jnp.where(lane == 16 * q + sub, jnp.sum(acc, axis=1, keepdims=True), 0.0)
     row = jnp.sum(packed, axis=0, keepdims=True)
 
+    def reorder(x, carry):
+        for y in range(8):
+            where = pl.ds(8 * x + y, NS, stride=XY)
+            zt_ref[where, :] = z_ref[x, y]
+            vt_ref[where, :] = v_ref[x, y]
+        return carry
+
+    store_z = pltpu.make_async_copy(zt_ref, zt_out, store_sem.at[1])
+    store_v = pltpu.make_async_copy(vt_ref, vt_out, store_sem.at[2])
     rows_sent = []
     slot = 0
     for phase, (count, peer) in enumerate(((ng, peer_g), (ny, peer_y), (nz, peer_z))):
@@ -582,6 +606,10 @@
             copy.start()
             copies.append((slot, copy))
             slot += 1
+        if phase == 0:
+            lax.fori_loop(0, 8, reorder, 0)
+            store_z.start()
+            store_v.start()
         for _, copy in copies:
             copy.wait_recv()
         for at, _ in copies:
@@ -595,17 +623,16 @@
     ratio = b / c
     gamma = (c - ratio * a) / (d - ratio * b)
     alpha = a / c - gamma * ratio
-    alpha = jnp.broadcast_to(alpha, (NS, 128))
-    gamma = jnp.broadcast_to(gamma, (NS, 128))
-
-    def finish(x, carry):
-        for y in range(8):
-            out_ref[pl.ds(8 * x + y, NS, stride=XY), :] = alpha * z_ref[x, y] + gamma * v_ref[x, y]
-        return carry
-
-    lax.fori_loop(0, 8, finish, 0)
+    alpha_ref[...] = jnp.broadcast_to(alpha, (NS, 128))
+    gamma_ref[...] = jnp.broadcast_to(gamma, (NS, 128))
+
+    for _, _, copy in started:
+        copy.wait_send()
     for copy in rows_sent:
         copy.wait_send()
+    store_div.wait()
+    store_z.wait()
+    store_v.wait()
 
 
 def shards(nz, ny, ng, *args):
@@ -626,14 +653,20 @@
         jnp.asarray(slope_table()),
     ]
     cube = pltpu.VMEM((8, 8, NS, 128), F32)
-    out, div = pl.pallas_call(
+    zt, vt, div, alpha, gamma = pl.pallas_call(
         functools.partial(kernel, nz, ny, ng),
         out_shape=(
             jax.ShapeDtypeStruct((NS * XY, 128), F32),
+            jax.ShapeDtypeStruct((NS * XY, 128), F32),
             jax.ShapeDtypeStruct((XY, 128), F32),
+            jax.ShapeDtypeStruct((NS, 128), F32),
+            jax.ShapeDtypeStruct((NS, 128), F32),
         ),
         in_specs=[pl.BlockSpec(memory_space=pltpu.HBM)] * 12,
         out_specs=(
+            pl.BlockSpec(memory_space=pltpu.HBM),
+            pl.BlockSpec(memory_space=pltpu.HBM),
+            pl.BlockSpec(memory_space=pltpu.HBM),
             pl.BlockSpec(memory_space=pltpu.VMEM),
             pl.BlockSpec(memory_space=pltpu.VMEM),
         ),
@@ -648,26 +681,30 @@
         ]
         + [cube] * 8
         + [
-            pltpu.VMEM((2, 4, 136, 128), F32),
-            pltpu.VMEM((2, 4, 24, 128), F32),
-            pltpu.VMEM((2, 4, 136, 128), F32),
-            pltpu.VMEM((2, 4, 24, 128), F32),
-            pltpu.VMEM((4, 8, NS, 128), F32),
-            pltpu.VMEM((4, NS, 128), F32),
+            pltpu.VMEM((3, 4, 8, NS, 128), F32),
+            pltpu.VMEM((3, 4, NS, 128), F32),
+            pltpu.VMEM((8, NS, 128), F32),
+            pltpu.VMEM((8, NS, 128), F32),
+            pltpu.VMEM((XY, 128), F32),
+            pltpu.VMEM((NS * XY, 128), F32),
+            pltpu.VMEM((NS * XY, 128), F32),
             pltpu.VMEM((3, 1, 128), F32),
             pltpu.VMEM((count, 1, 128), F32),
             pltpu.SemaphoreType.DMA((12,)),
-            pltpu.SemaphoreType.DMA((24,)),
-            pltpu.SemaphoreType.DMA((24,)),
+            pltpu.SemaphoreType.DMA((3,)),
+            pltpu.SemaphoreType.DMA((32,)),
+            pltpu.SemaphoreType.DMA((32,)),
             pltpu.SemaphoreType.DMA((count,)),
             pltpu.SemaphoreType.DMA((count,)),
         ],
         compiler_params=pltpu.CompilerParams(
-            collective_id=0, has_side_effects=True, vmem_limit_bytes=40 * 1024 * 1024
+            collective_id=0, has_side_effects=True, vmem_limit_bytes=67043328
         ),
         name="reacting_step",
     )(*operands)
-    return out.reshape(NS, 8, 8, 128), div.reshape(8, 8, 128)
+    zt, vt = zt.reshape(NS, 8, 8, 128), vt.reshape(NS, 8, 8, 128)
+    out = alpha[:, None, None, :] * zt + gamma[:, None, None, :] * vt
+    return out, div.reshape(8, 8, 128)
 
 
 def solution(mesh):

time: 59.9 us -> 52 us (0.87)
  local copies, waits for them, and re-layouts: 9.45 us -> 1.31 us
  other arithmetic: 0 us -> 2.09 us
  Pallas kernels: 49 us -> 47.5 us
    unnamed x26 -> x5, local copies, waits for them, and re-layouts: 9.45 us -> 1.31 us
    add x0 -> x1, other arithmetic: none -> 2.09 us  [shards(): out = alpha[:, None, None, :] * zt + gamma[:, None, None, :] * vt]
    pallas_call x1, Pallas kernels: 49 us -> 47.5 us  [shards(): pl.pallas_call(functools.partial(kernel, nz, ny, ng), out_shape=(jax.Shap...]
where the time goes in v3:
time: 52 us; the launch traced here: 51.6 us
  Pallas kernels  47.5 us (91%)
  other arithmetic  2.09 us (4%)
  local copies, waits for them, and re-layouts  1.31 us (3%)
  between operations  0.65 us (1%)
    pallas_call x1, Pallas kernels, shards(): pl.pallas_call(functools.partial(kernel, nz, ny, ng), out_shape=(jax.Shap...  47.5 us
    add x1, other arithmetic, shards(): out = alpha[:, None, None, :] * zt + gamma[:, None, None, :] * vt  2.09 us
    unnamed x5, local copies, waits for them, and re-layouts  1.31 us

profile of v3, /device:TPU:1, one launch (start us, length us, event | category | flops | bytes accessed | tf_op | source)
XLA Modules:
  0.0 51.6 jit_solution(16411881980061432269)
XLA Ops:
  0.6 47.5 %reacting_step.1 = (f32[1024,128]{1,0:T(8,128)}, f32[1024,128]{1,0:T(8,128)}, f32[64,128]{1,0:T(8,128)}, f32[16,128]{1,0:T(8,128)}, f32[16,128]{1,0:T(8,128)}) custom-call(f32[2048,128]{1,0:T(8,128)} %bitcast.12, f32[64,128]{1,0:T(8,128)} %bitcast.15, f32[64,128]{1,0:T(8,128)} %bitcast.16, f32[1,16]{1,0:T(1,128)} %bitcast.19, f32[1,16]{1,0:T(1,128)} %bitcast.20, ...), custom_call_target="tpu_custom_call" | custom-call | tf_op jit(solution)/shard_map/reacting_step/pallas_call | solution.py:656
  48.2 0.0 copy-start.1
  48.2 0.7 %copy-done.1 = f32[16,128]{1,0:T(8,128)S(1)} copy-done((f32[16,128]{1,0:T(8,128)S(1)}, f32[16,128]{1,0:T(8,128)}, u32[]{:S(2)}) %copy-start.1) | copy-done | bytes 8216
  48.9 0.0 copy-start
  48.9 2.1 %multiply_add_fusion = f32[16,8,8,128]{3,2,1,0:T(8,128)} fusion(f32[16,8,8,128]{3,2,1,0:T(8,128)} %bitcast.14, f32[16,8,8,128]{3,2,1,0:T(8,128)} %bitcast.13, f32[16,128]{1,0:T(8,128)} %get-tuple-element.9, f32[16,128]{1,0:T(8,128)S(1)} %copy-done.1), kind=kLoop, calls=%fused_computation | loop fusion | flops 393216 | bytes 1589248 | tf_op jit(solution)/shard_map/add | solution.py:706
  51.0 0.0 copy-done
  51.0 0.6 %copy.15 = f32[8,8,128]{2,1,0:T(8,128)} copy(f32[8,8,128]{2,1,0:T(8,128)S(1)} %bitcast.17) | data formatting | bytes 65536
Async XLA Ops:
  48.2 0.7 %copy-start.1 = (f32[16,128]{1,0:T(8,128)S(1)}, f32[16,128]{1,0:T(8,128)}, u32[]{:S(2)}) copy-start(f32[16,128]{1,0:T(8,128)} %get-tuple-element.7) | copy-start | bytes 24580
  48.9 2.1 %copy-start = (f32[64,128]{1,0:T(8,128)S(1)}, f32[64,128]{1,0:T(8,128)}, u32[]{:S(2)}) copy-start(f32[64,128]{1,0:T(8,128)} %get-tuple-element.11) | copy-start | bytes 98308

commit v4 on v3

--- a/solution.py
+++ b/solution.py
@@ -371,12 +371,6 @@
             total = here[16:17] + here[17:18] + here[18:19]
             div_ref[pl.ds(at, 1), :] = total * g_ref[3, pl.ds(at, 1), :]
 
-    def chem_sides(i, carry):
-        for j in range(2):
-            x = 4 * i + 2 * j
-            chem([(x, 0), (x, 7), (x + 1, 0), (x + 1, 7)], False)
-        return carry
-
     def chem_inside(i, carry):
         for j in range(2):
             chem([(1 + 2 * i + j, y) for y in range(1, 7)], True)
@@ -390,12 +384,22 @@
     pl.semaphore_wait(barrier, len(greeted))
     for d in range(8):
         send(0, d, my_ref)
-    chem([(0, y) for y in range(1, 7)], False)
-    chem([(7, y) for y in range(1, 7)], False)
-    lax.fori_loop(0, 2, chem_sides, 0)
-    for d in range(8):
+    def chem_ends(i, carry):
+        chem([(7 * i, y) for y in range(4)], False)
+        chem([(7 * i, y) for y in range(4, 8)], False)
+        return carry
+
+    def chem_sides(i, carry):
+        chem([(1 + i, 0), (1 + i, 7), (4 + i, 0), (4 + i, 7)], False)
+        return carry
+
+    lax.fori_loop(0, 2, chem_ends, 0)
+    for d in (4, 5, 6, 7, 0, 1):
         send_scalars(d)
-    for d in range(8):
+        send(1, d, mp_ref)
+    lax.fori_loop(0, 3, chem_sides, 0)
+    for d in (2, 3):
+        send_scalars(d)
         send(1, d, mp_ref)
     lax.fori_loop(0, 3, chem_inside, 0)
 
@@ -422,6 +426,22 @@
 
     def flat_zsum(value):
         return zsum(value.reshape(-1, 128)).reshape(value.shape)
+
+    fetch[11].wait()
+
+    def slope_product(value, which):
+        first, second, third = pieces(value)
+        wide = jnp.dot(
+            jnp.concatenate([first, second], axis=1),
+            slopes[which, :, 0:256],
+            preferred_element_type=F32,
+        )
+        thin = jnp.dot(
+            jnp.concatenate([first, third], axis=1),
+            slopes[which, :, 256:384],
+            preferred_element_type=F32,
+        )
+        return wide[:, 0:128] + wide[:, 128:256] + thin
 
     def begin(x, y, step, count, made, carried, acc):
         first, jump = 8 * x + y, 8 * step[0] + step[1]
@@ -440,7 +460,7 @@
         precond = inv * resid
         for i, (a, b) in enumerate(spots):
             z_ref[a, b] = precond[i]
-        return acc + jnp.sum(resid * precond * part, axis=0)
+        return acc + jnp.sum(resid * precond * part, axis=0), precond
 
     def advance(x, y, step, count, image, acc):
         first, jump = 8 * x + y, 8 * step[0] + step[1]
@@ -456,7 +476,7 @@
         precond = inv * image
         for i, (a, b) in enumerate(spots):
             v_ref[a, b] = precond[i]
-        return acc + jnp.sum(image * precond * part, axis=0)
+        return acc + jnp.sum(image * precond * part, axis=0), precond
 
     def with_edges(field, stage, x, y, step, count):
         spots = [(x + i * step[0], y + i * step[1]) for i in range(count)]
@@ -467,55 +487,53 @@
     store_div = pltpu.make_async_copy(divout_ref, div_out, store_sem.at[0])
     store_div.start()
 
+    def z_stiff(values, weights):
+        flat = values.reshape(-1, 128)
+        back = slope_product(slope_product(flat, 0) * weights.reshape(-1, 128), 1)
+        return back.reshape(values.shape)
+
     def begin_inside(i, acc):
-        x = 1 + i
-        return begin(x, 1, (0, 1), 6, mp_ref[x, 1:7], my_ref[x, 1:7], acc)
-
-    dot_a = lax.fori_loop(0, 6, begin_inside, none)
+        planes = []
+        for j in range(2):
+            x = 1 + 2 * i + j
+            acc, precond = begin(x, 1, (0, 1), 6, mp_ref[x, 1:7], my_ref[x, 1:7], acc)
+            planes.append(precond)
+        first = 1 + 2 * i
+        weights = jnp.concatenate([wb_ref[first, 1:7], wb_ref[first + 1, 1:7]], axis=0)
+        back = z_stiff(jnp.concatenate(planes, axis=0), weights)
+        y_ref[first, 1:7] = back[0:6]
+        y_ref[first + 1, 1:7] = back[6:12]
+        return acc
+
+    def edge_spots():
+        return [(x + i * step[0], y + i * step[1]) for x, y, step, count in EDGES for i in range(count)]
+
+    dot_a = lax.fori_loop(0, 3, begin_inside, none)
     await_from(0, range(8))
     await_from(1, range(8))
+    values = []
     for x, y, step, count in EDGES:
         made = with_edges(mp_ref, 1, x, y, step, count)
         carried = with_edges(my_ref, 0, x, y, step, count)
-        dot_a = begin(x, y, step, count, made, carried, dot_a)
-
-    fetch[11].wait()
-
-    def slope_product(value, which):
-        first, second, third = pieces(value)
-        wide = jnp.dot(
-            jnp.concatenate([first, second], axis=1),
-            slopes[which, :, 0:256],
-            preferred_element_type=F32,
-        )
-        thin = jnp.dot(
-            jnp.concatenate([first, third], axis=1),
-            slopes[which, :, 256:384],
-            preferred_element_type=F32,
-        )
-        return wide[:, 0:128] + wide[:, 128:256] + thin
-
-    def yz_part(planes, weights):
-        value = jnp.concatenate([p.reshape(128, 128) for p in planes], axis=0)
-        weight = jnp.concatenate([w.reshape(128, 128) for w in weights], axis=0)
-        back = slope_product(slope_product(value, 0) * weight, 1)
-        result = []
-        for i, (p, w) in enumerate(zip(planes, weights)):
-            lines = jnp.stack(stiff_line([p[y] for y in range(8)], [w[y] for y in range(8)]))
-            result.append(back[128 * i : 128 * (i + 1)].reshape(8, NS, 128) + lines)
-        return result
+        dot_a, precond = begin(x, y, step, count, made, carried, dot_a)
+        values.append(precond)
+    weights = jnp.stack([wb_ref[x, y] for x, y in edge_spots()])
+    back = z_stiff(jnp.concatenate(values, axis=0), weights)
+    for i, (x, y) in enumerate(edge_spots()):
+        y_ref[x, y] = back[i]
+
+    def y_lines(plane, weight):
+        return jnp.stack(stiff_line([plane[y] for y in range(8)], [weight[y] for y in range(8)]))
 
     def operate(source, faces_done):
-        planes = [source[0], source[7]]
-        got = yz_part(planes, [wb_ref[0], wb_ref[7]])
-        y_ref[0] = got[0]
-        y_ref[7] = got[1]
+        for x in (0, 7):
+            y_ref[x] = y_ref[x] + y_lines(source[x], wb_ref[x])
 
         def x_part(y, acc):
             values = [source[x, y] for x in range(8)]
             got = stiff_line(values, [wb_ref[x, y] for x in range(8)])
             for x in range(1, 7):
-                y_ref[x, y] = got[x]
+                y_ref[x, y] = y_ref[x, y] + got[x]
             for x in (0, 7):
                 image = diff * (y_ref[x, y] + got[x]) + hm_ref[x, y] * values[x]
                 y_ref[x, y] = image
@@ -526,13 +544,12 @@
         faces_done()
 
         def rest_part(i, acc):
-            first = 1 + 2 * i
-            planes = [source[first], source[first + 1]]
-            got = yz_part(planes, [wb_ref[first], wb_ref[first + 1]])
             for j in range(2):
-                image = diff * (y_ref[first + j] + got[j]) + hm_ref[first + j] * planes[j]
-                y_ref[first + j] = image
-                acc = acc + jnp.sum(planes[j] * image, axis=0)
+                x = 1 + 2 * i + j
+                plane = source[x]
+                image = diff * (y_ref[x] + y_lines(plane, wb_ref[x])) + hm_ref[x] * plane
+                y_ref[x] = image
+                acc = acc + jnp.sum(plane * image, axis=0)
             return acc
 
         return lax.fori_loop(0, 3, rest_part, total)
@@ -545,33 +562,44 @@
     for d in (2, 3):
         send(2, d, y_ref)
 
-    def advance_inside(i, acc):
-        x = 1 + i
-        return advance(x, 1, (0, 1), 6, y_ref[x, 1:7], acc)
-
-    dot_b = lax.fori_loop(0, 6, advance_inside, none)
+    def z_square(values, weights):
+        slope = slope_product(values.reshape(-1, 128), 0).reshape(values.shape)
+        return jnp.sum(weights * slope * slope, axis=0)
+
+    def advance_inside(i, accs):
+        acc, stiff = accs
+        planes = []
+        for j in range(2):
+            x = 1 + 2 * i + j
+            acc, precond = advance(x, 1, (0, 1), 6, y_ref[x, 1:7], acc)
+            planes.append(precond)
+        first = 1 + 2 * i
+        weights = jnp.concatenate([wb_ref[first, 1:7], wb_ref[first + 1, 1:7]], axis=0)
+        return acc, stiff + z_square(jnp.concatenate(planes, axis=0), weights)
+
+    dot_b, stiff = lax.fori_loop(0, 3, advance_inside, (none, none))
     await_from(2, range(8))
+    values = []
     for x, y, step, count in EDGES:
-        dot_b = advance(x, y, step, count, with_edges(y_ref, 2, x, y, step, count), dot_b)
+        dot_b, precond = advance(x, y, step, count, with_edges(y_ref, 2, x, y, step, count), dot_b)
+        values.append(precond)
+    weights = jnp.stack([wb_ref[x, y] for x, y in edge_spots()])
+    stiff = stiff + z_square(jnp.concatenate(values, axis=0), weights)
 
     def square_x(y, acc):
         slopes_x = apply_line([v_ref[x, y] for x in range(8)], FORWARD)
         return acc + sum(wb_ref[x, y] * slopes_x[x] * slopes_x[x] for x in range(8))
 
-    def square_yz(i, accs):
+    def square_y(i, accs):
         acc, mass = accs
-        first = 2 * i
-        value = v_ref[pl.ds(first, 2)].reshape(256, 128)
-        slope_z = slope_product(value, 0)
         for j in range(2):
-            plane, weight = v_ref[first + j], wb_ref[first + j]
+            plane, weight = v_ref[2 * i + j], wb_ref[2 * i + j]
             slope_y = jnp.stack(apply_line([plane[y] for y in range(8)], FORWARD))
-            here = slope_z[128 * j : 128 * (j + 1)].reshape(8, NS, 128)
-            acc = acc + jnp.sum(weight * (slope_y * slope_y + here * here), axis=0)
-            mass = mass + jnp.sum(hm_ref[first + j] * plane * plane, axis=0)
+            acc = acc + jnp.sum(weight * slope_y * slope_y, axis=0)
+            mass = mass + jnp.sum(hm_ref[2 * i + j] * plane * plane, axis=0)
         return acc, mass
 
-    stiff, mass = lax.fori_loop(0, 4, square_yz, (none, none))
+    stiff, mass = lax.fori_loop(0, 4, square_y, (stiff, none))
     stiff = lax.fori_loop(0, 8, square_x, stiff)
     dot_d = diff * stiff + mass
 
@@ -633,6 +661,43 @@
     store_div.wait()
     store_z.wait()
     store_v.wait()
+
+
+def combine(zt, vt, alpha, gamma, div, out, div_out, *scratch):
+    z_ref, v_ref, o_ref, a_ref, g_ref, d_ref, in_sem, out_sem = scratch
+    small = [
+        pltpu.make_async_copy(alpha, a_ref, in_sem.at[8]),
+        pltpu.make_async_copy(gamma, g_ref, in_sem.at[9]),
+        pltpu.make_async_copy(div, d_ref, in_sem.at[10]),
+    ]
+    for one in small:
+        one.start()
+    parts = [slice(256 * i, 256 * i + 256) for i in range(4)]
+    come = []
+    for i, part in enumerate(parts):
+        come.append(
+            (
+                pltpu.make_async_copy(zt.at[part], z_ref.at[part], in_sem.at[2 * i]),
+                pltpu.make_async_copy(vt.at[part], v_ref.at[part], in_sem.at[2 * i + 1]),
+            )
+        )
+        for one in come[i]:
+            one.start()
+    for one in small:
+        one.wait()
+    leave = [pltpu.make_async_copy(d_ref, div_out, out_sem.at[4])]
+    leave[0].start()
+    for i, part in enumerate(parts):
+        for one in come[i]:
+            one.wait()
+        for j in range(4):
+            s = 4 * i + j
+            here = slice(XY * s, XY * s + XY)
+            o_ref[here, :] = a_ref[s : s + 1, :] * z_ref[here, :] + g_ref[s : s + 1, :] * v_ref[here, :]
+        leave.append(pltpu.make_async_copy(o_ref.at[part], out.at[part], out_sem.at[i]))
+        leave[-1].start()
+    for one in leave:
+        one.wait()
 
 
 def shards(nz, ny, ng, *args):
@@ -702,9 +767,32 @@
         ),
         name="reacting_step",
     )(*operands)
-    zt, vt = zt.reshape(NS, 8, 8, 128), vt.reshape(NS, 8, 8, 128)
-    out = alpha[:, None, None, :] * zt + gamma[:, None, None, :] * vt
-    return out, div.reshape(8, 8, 128)
+    whole = pltpu.VMEM((NS * XY, 128), F32)
+    out, div = pl.pallas_call(
+        combine,
+        out_shape=(
+            jax.ShapeDtypeStruct((NS * XY, 128), F32),
+            jax.ShapeDtypeStruct((XY, 128), F32),
+        ),
+        in_specs=[pl.BlockSpec(memory_space=pltpu.HBM)] * 5,
+        out_specs=(
+            pl.BlockSpec(memory_space=pltpu.HBM),
+            pl.BlockSpec(memory_space=pltpu.HBM),
+        ),
+        scratch_shapes=[
+            whole,
+            whole,
+            whole,
+            pltpu.VMEM((NS, 128), F32),
+            pltpu.VMEM((NS, 128), F32),
+            pltpu.VMEM((XY, 128), F32),
+            pltpu.SemaphoreType.DMA((11,)),
+            pltpu.SemaphoreType.DMA((5,)),
+        ],
+        compiler_params=pltpu.CompilerParams(vmem_limit_bytes=67043328),
+        name="combine",
+    )(zt, vt, alpha, gamma, div)
+    return out.reshape(NS, 8, 8, 128), div.reshape(8, 8, 128)
 
 
 def solution(mesh):

time: 52 us -> 50.8 us (0.977)
  Pallas kernels: 47.5 us -> 50 us
  other arithmetic: 2.09 us -> 0 us
  local copies, waits for them, and re-layouts: 1.31 us -> 0 us
    pallas_call x0 -> x1, Pallas kernels: none -> 2.14 us  [shards(): pl.pallas_call(combine, out_shape=(jax.ShapeDtypeStruct((NS * XY, 128), F...]
    add x1 -> x0, other arithmetic: 2.09 us -> none  [shards(): out = alpha[:, None, None, :] * zt + gamma[:, None, None, :] * vt]
    unnamed x5 -> x0, local copies, waits for them, and re-layouts: 1.31 us -> none
where the time goes in v4:
time: 50.8 us; the launch traced here: 50.6 us
  Pallas kernels  50 us (98%)
  between operations  0.64 us (1%)
    pallas_call x1, Pallas kernels, shards(): pl.pallas_call(functools.partial(kernel, nz, ny, ng), out_shape=(jax.Shap...  47.8 us
    pallas_call x1, Pallas kernels, shards(): pl.pallas_call(combine, out_shape=(jax.ShapeDtypeStruct((NS * XY, 128), F...  2.14 us

profile of v4, /device:TPU:1, one launch (start us, length us, event | category | flops | bytes accessed | tf_op | source)
XLA Modules:
  0.0 50.6 jit_solution(7687334300454851750)
XLA Ops:
  0.6 47.8 %reacting_step.1 = (f32[1024,128]{1,0:T(8,128)}, f32[1024,128]{1,0:T(8,128)}, f32[64,128]{1,0:T(8,128)}, f32[16,128]{1,0:T(8,128)}, f32[16,128]{1,0:T(8,128)}) custom-call(f32[2048,128]{1,0:T(8,128)} %bitcast.11, f32[64,128]{1,0:T(8,128)} %bitcast.12, f32[64,128]{1,0:T(8,128)} %bitcast.13, f32[1,16]{1,0:T(1,128)} %bitcast.15, f32[1,16]{1,0:T(1,128)} %bitcast.16, ...), custom_call_target="tpu_custom_call" | custom-call | tf_op jit(solution)/shard_map/reacting_step/pallas_call | solution.py:721
  48.5 2.1 %combine.1 = (f32[1024,128]{1,0:T(8,128)}, f32[64,128]{1,0:T(8,128)}) custom-call(f32[1024,128]{1,0:T(8,128)} %get-tuple-element.9.zt, f32[1024,128]{1,0:T(8,128)} %get-tuple-element.10.vt, f32[16,128]{1,0:T(8,128)} %get-tuple-element.11.alpha, f32[16,128]{1,0:T(8,128)} %get-tuple-element.12.gamma, f32[64,128]{1,0:T(8,128)} %get-tuple-element.13.div), custom_call_target="tpu_custom_call" | custom-call | tf_op jit(solution)/shard_map/combine/pallas_call | solution.py:771

commit v5 on v4

--- a/solution.py
+++ b/solution.py
@@ -578,9 +578,11 @@
         return acc, stiff + z_square(jnp.concatenate(planes, axis=0), weights)
 
     dot_b, stiff = lax.fori_loop(0, 3, advance_inside, (none, none))
-    await_from(2, range(8))
+    await_from(2, (2, 3))
     values = []
     for x, y, step, count in EDGES:
+        if x == 0:
+            await_from(2, (0, 1, 4, 5, 6, 7))
         dot_b, precond = advance(x, y, step, count, with_edges(y_ref, 2, x, y, step, count), dot_b)
         values.append(precond)
     weights = jnp.stack([wb_ref[x, y] for x, y in edge_spots()])
@@ -619,10 +621,10 @@
     store_v = pltpu.make_async_copy(vt_ref, vt_out, store_sem.at[2])
     rows_sent = []
     slot = 0
-    for phase, (count, peer) in enumerate(((ng, peer_g), (ny, peer_y), (nz, peer_z))):
+    for phase, (count, peer) in enumerate(((ng, peer_g), (nz, peer_z), (ny, peer_y))):
         srow[phase] = row
         copies = []
-        for k in range(1, count):
+        for k in sorted(range(1, count), key=lambda k: -min(k, count - k)):
             copy = pltpu.make_async_remote_copy(
                 src_ref=srow.at[phase],
                 dst_ref=rrow.at[slot],

time: 50.8 us -> 50.7 us (level)
  no operation moved by 1% of the time
where the time goes in v5:
time: 50.7 us; the launch traced here: 50.5 us
  Pallas kernels  49.9 us (98%)
  between operations  0.64 us (1%)
    pallas_call x1, Pallas kernels, shards(): pl.pallas_call(functools.partial(kernel, nz, ny, ng), out_shape=(jax.Shap...  47.7 us
    pallas_call x1, Pallas kernels, shards(): pl.pallas_call(combine, out_shape=(jax.ShapeDtypeStruct((NS * XY, 128), F...  2.14 us

profile of v5, /device:TPU:1, one launch (start us, length us, event | category | flops | bytes accessed | tf_op | source)
XLA Modules:
  0.0 50.5 jit_solution(4991809663017400588)
XLA Ops:
  0.6 47.7 %reacting_step.1 = (f32[1024,128]{1,0:T(8,128)}, f32[1024,128]{1,0:T(8,128)}, f32[64,128]{1,0:T(8,128)}, f32[16,128]{1,0:T(8,128)}, f32[16,128]{1,0:T(8,128)}) custom-call(f32[2048,128]{1,0:T(8,128)} %bitcast.11, f32[64,128]{1,0:T(8,128)} %bitcast.12, f32[64,128]{1,0:T(8,128)} %bitcast.13, f32[1,16]{1,0:T(1,128)} %bitcast.15, f32[1,16]{1,0:T(1,128)} %bitcast.16, ...), custom_call_target="tpu_custom_call" | custom-call | tf_op jit(solution)/shard_map/reacting_step/pallas_call | solution.py:723
  48.4 2.1 %combine.1 = (f32[1024,128]{1,0:T(8,128)}, f32[64,128]{1,0:T(8,128)}) custom-call(f32[1024,128]{1,0:T(8,128)} %get-tuple-element.9.zt, f32[1024,128]{1,0:T(8,128)} %get-tuple-element.10.vt, f32[16,128]{1,0:T(8,128)} %get-tuple-element.11.alpha, f32[16,128]{1,0:T(8,128)} %get-tuple-element.12.gamma, f32[64,128]{1,0:T(8,128)} %get-tuple-element.13.div), custom_call_target="tpu_custom_call" | custom-call | tf_op jit(solution)/shard_map/combine/pallas_call | solution.py:773
